TPU v7x, 256 devices: a whole 4x4x8 slice. The times are simulated.
256 devices in a mesh: leaf: 4 (over y), row: 16 (over z, core), col: 4 (over x).
Axes of the slice: x: 4, y: 4, z: 8, core: 2. Of those that a mesh axis runs over, the one named last changes fastest.
Arguments:
- anc_inverse: float32 [24, 24, 512, 512], P('leaf', None, 'row', 'col'), may hold values from -6 to 6, as said below
- struct_one: int32 [12, 5], P('leaf'), may hold values from 0 to 23, as said below
- lower_one: float32 [12, 5, 512, 512], P('leaf', None, 'row', 'col'), may hold values from -0.125 to 0.125
- pivot_inv_one: float32 [12, 512, 512], P('leaf', 'row', 'col'), may hold values from -6 to 6, as said below
- lower_two: float32 [24, 6, 512, 512], P('leaf', None, 'row', 'col'), may hold values from -0.109375 to 0.109375
- pivot_inv_two: float32 [24, 512, 512], P('leaf', 'row', 'col'), may hold values from -6 to 6, as said below
Outputs:
- offdiag_one: float32 [12, 5, 512, 512], P('leaf', None, 'row', 'col')
- diag_one: float32 [12, 512, 512], P('leaf', 'row', 'col')
- offdiag_two: float32 [24, 6, 512, 512], P('leaf', None, 'row', 'col')
- diag_two: float32 [24, 512, 512], P('leaf', 'row', 'col')
Inputs may be any that keep to these rules, and one draw needn't show every extreme that they name: `struct_one`: each row lists 5 different separator block numbers in increasing order. symmetric: anc_inverse[b, a] is the transpose of anc_inverse[a, b]. `pivot_inv_one`: every block equals its transpose. `pivot_inv_two`: every block equals its transpose.
All inputs are finite; a program needn't handle non-finite values.
Results may differ from a plain program's by a relative error of at most 0.0001.
Values sent between devices are 32-bit elements; how exact they have to be, the bound alone decides.
A program may use at most 64 MiB of HBM per device.

v0:
```python
import jax
import jax.numpy as jnp
from jax import lax
from jax.sharding import PartitionSpec as P

highest = lax.Precision.HIGHEST


def on_device(anc_inverse, struct_one, lower_one, pivot_inv_one, lower_two, pivot_inv_two):
    level_nodes, struct_len = struct_one.shape
    tile_rows = lower_one.shape[2]
    tile_cols = lower_one.shape[3]
    children = lower_two.shape[0] // level_nodes
    one_rows = lax.all_gather(lower_one, "row", axis=2, tiled=True)
    one_cols, two_cols = (
        lax.all_gather(lower_one, "col", axis=3, tiled=True),
        lax.all_gather(lower_two, "col", axis=3, tiled=True),
    )
    ancestors = lax.all_gather(anc_inverse, "leaf", axis=0, tiled=True)
    selected = ancestors[struct_one[:, :, None], struct_one[:, None, :]]
    stripes = lax.all_gather(selected, "col", axis=4, tiled=True)
    offdiag_one = -jnp.einsum("mstik,mtkj->msij", stripes, one_rows, precision=highest)
    cols_piece = one_cols
    summed_one = lax.psum_scatter(
        jnp.einsum("mski,mskj->imj", cols_piece, offdiag_one, precision=highest),
        "row",
        scatter_dimension=0,
        tiled=True,
    )
    diag_one = pivot_inv_one - jnp.transpose(summed_one, (1, 0, 2))
    parent_col = jnp.concatenate([offdiag_one, diag_one[:, None]], axis=1)
    parent_stripe = lax.all_gather(parent_col, "col", axis=3, tiled=True)
    two_rows = lax.all_gather(lower_two, "row", axis=2, tiled=True)
    rows_split = two_rows.reshape(
        level_nodes, children, struct_len + 1, two_rows.shape[2], tile_cols
    )
    cols_split = two_cols.reshape(
        level_nodes, children, struct_len + 1, tile_rows, two_cols.shape[3]
    )
    local_split = lower_two.reshape(level_nodes, children, struct_len + 1, tile_rows, tile_cols)
    upper_part = jnp.einsum(
        "mstik,mctkj->mcsij", stripes, rows_split[:, :, :struct_len], precision=highest
    )
    upper_part = upper_part + jnp.einsum(
        "msik,mckj->mcsij",
        parent_stripe[:, :struct_len],
        rows_split[:, :, struct_len],
        precision=highest,
    )
    stripe_piece = parent_stripe[:, :struct_len]
    summed_parent = lax.psum_scatter(
        jnp.einsum(
            "mqki,mcqkj->imcj", stripe_piece, local_split[:, :, :struct_len], precision=highest
        ),
        "row",
        scatter_dimension=0,
        tiled=True,
    )
    parent_row = jnp.transpose(summed_parent, (1, 2, 0, 3))
    parent_row = parent_row + jnp.einsum(
        "mik,mckj->mcij",
        parent_stripe[:, struct_len],
        rows_split[:, :, struct_len],
        precision=highest,
    )
    offdiag_split = -jnp.concatenate([upper_part, parent_row[:, :, None]], axis=2)
    cols_piece = cols_split
    summed_two = lax.psum_scatter(
        jnp.einsum("mcpki,mcpkj->imcj", cols_piece, offdiag_split, precision=highest),
        "row",
        scatter_dimension=0,
        tiled=True,
    )
    diag_two = pivot_inv_two - jnp.transpose(summed_two, (1, 2, 0, 3)).reshape(
        level_nodes * children, tile_rows, tile_cols
    )
    offdiag_two = offdiag_split.reshape(
        level_nodes * children, struct_len + 1, tile_rows, tile_cols
    )
    return (offdiag_one, diag_one, offdiag_two, diag_two)


def solution(mesh):
    placed = (
        P("leaf", None, "row", "col"),
        P("leaf", None),
        P("leaf", None, "row", "col"),
        P("leaf", "row", "col"),
        P("leaf", None, "row", "col"),
        P("leaf", "row", "col"),
    )
    return jax.shard_map(
        on_device,
        mesh=mesh,
        in_specs=placed,
        out_specs=(
            P("leaf", None, "row", "col"),
            P("leaf", "row", "col"),
            P("leaf", None, "row", "col"),
            P("leaf", "row", "col"),
        ),
        check_vma=False,
    )
```

profile of v0, /device:TPU:1, one launch (start us, length us, event | category | flops | bytes accessed | tf_op | source)
XLA Modules:
  0.0 604.5 jit_solution(8348671050504362168)
XLA Ops:
  7.2 0.0 copy-start.7
  7.2 0.0 all-gather.7.cloned.1.call-start
  7.2 0.7 all-gather.7.cloned.1.call-update
  7.9 0.0 copy-start.3
  7.9 0.0 all-gather.11.cloned.1.call-start
  8.0 0.7 all-gather.11.cloned.1.call-update
  8.7 0.0 all-gather.9.cloned.1.call-start
  8.7 0.0 copy-done.7
  8.7 0.1 broadcast_or_fusion
  8.8 0.1 reshape.41
  8.9 99.3 %all-gather.7.cloned.1.call-done = f32[24,24,32,128]{3,2,1,0:T(8,128)} async-done(((f32[6,24,32,128]{3,2,1,0:T(8,128)}), f32[24,24,32,128]{3,2,1,0:T(8,128)}) %all-gather.7.cloned.1.call-update) | async-done | bytes 9437200 | tf_op jit(solution)/shard_map/all_gather | solution.py:19
  108.2 5.9 gather_fusion
  114.1 0.0 all-gather.9.cloned.1.call-update
  114.1 0.0 reduce-scatter.3.cloned.1.call-start
  114.2 0.0 copy-done.3
  114.2 13.2 %all_gather.24 = f32[3,5,32,512]{3,2,1,0:T(8,128)S(1)} all-gather(f32[3,5,32,128]{3,2,1,0:T(8,128)S(1)} %copy-done.3), channel_id=1, replica_groups=mesh['leaf'=4,'row'=16,'col'=4] {'col'}, dimensions={3}, use_global_device_ids=true | all-gather | bytes 1228800 | tf_op jit(solution)/shard_map/all_gather | solution.py:16
  127.4 26.1 %all-gather.11.cloned.1.call-done = f32[3,5,512,128]{3,2,1,0:T(8,128)} async-done(((f32[3,5,32,128]{3,2,1,0:T(8,128)}), f32[3,5,512,128]{3,2,1,0:T(8,128)}) %all-gather.11.cloned.1.call-update) | async-done | bytes 3932176 | tf_op jit(solution)/shard_map/all_gather | solution.py:14
  153.5 59.6 %all-gather.9.cloned.1.call-done = f32[3,5,5,32,512]{4,3,2,1,0:T(8,128)} async-done(((f32[3,5,5,32,128]{4,3,2,1,0:T(8,128)}), f32[3,5,5,32,512]{4,3,2,1,0:T(8,128)}) %all-gather.9.cloned.1.call-update) | async-done | bytes 4915216 | tf_op jit(solution)/shard_map/all_gather | solution.py:21
  213.1 8.0 %fusion.22 = f32[3,5,32,128]{3,2,1,0:T(8,128)S(1)} fusion(f32[3,5,5,32,512]{4,3,2,1,0:T(8,128)} %all-gather.9.cloned.1.call-done, f32[3,5,512,128]{3,2,1,0:T(8,128)} %all-gather.11.cloned.1.call-done), kind=kOutput, calls=%fused_computation.19 | convolution fusion | flops 1887498240 | bytes 9093120 | tf_op jit(solution)/shard_map/mstik,mtkj->msij/dot_general | solution.py:22
  221.1 0.0 copy-start.2
  221.1 0.0 copy-start.6
  221.1 0.0 copy-start
  221.1 3.6 convolution_bitcast_fusion.2
  224.7 0.0 reduce-scatter.3.cloned.1.call-update
  224.7 0.0 all-gather.15.cloned.1.call-start
  224.8 55.9 %reduce-scatter.3.cloned.1.call-done = f32[32,3,128]{2,0,1:T(8,128)} async-done(((f32[512,3,128]{2,0,1:T(8,128)}), f32[32,3,128]{2,0,1:T(8,128)}) %reduce-scatter.3.cloned.1.call-update) | async-done | bytes 49168 | tf_op jit(solution)/shard_map/reduce_scatter | solution.py:24
  280.7 0.0 copy-done.6
  280.7 0.8 bitcast_subtract_fusion.1
  281.5 0.0 copy-start.4
  281.5 0.7 pad_maximum_fusion
  282.3 0.0 all-gather.15.cloned.1.call-update
  282.3 0.0 all-gather.13.cloned.1.call-start
  282.4 0.5 all-gather.13.cloned.1.call-update
  282.9 0.0 reduce-scatter.5.cloned.1.call-start
  282.9 30.0 %all-gather.15.cloned.1.call-done = f32[3,6,32,512]{3,2,1,0:T(8,128)} async-done(((f32[3,6,32,128]{3,2,1,0:T(8,128)}), f32[3,6,32,512]{3,2,1,0:T(8,128)}) %all-gather.15.cloned.1.call-update) | async-done | bytes 1179664 | tf_op jit(solution)/shard_map/all_gather | solution.py:32
  312.9 0.0 copy-done
  312.9 5.1 convolution_bitcast_fusion.1
  318.0 0.0 copy-done.2
  318.0 0.0 reduce-scatter.5.cloned.1.call-update
  318.0 0.0 copy-done.4
  318.0 0.0 all-gather.17.cloned.1.call-start
  318.0 0.7 all-gather.17.cloned.1.call-update
  318.8 0.2 all-reduce.3.cloned.1.call-start
  319.0 59.0 %all-gather.13.cloned.1.call-done = f32[6,6,512,128]{3,2,1,0:T(8,128)} async-done(((f32[6,6,32,128]{3,2,1,0:T(8,128)}), f32[6,6,512,128]{3,2,1,0:T(8,128)}) %all-gather.13.cloned.1.call-update) | async-done | bytes 9437200 | tf_op jit(solution)/shard_map/all_gather | solution.py:33
  377.9 0.0 copy-start.1
  378.0 10.1 %fusion.10 = f32[3,5,32,2,128]{4,2,3,1,0:T(8,128)S(1)} fusion(f32[3,2,6,512,128]{4,3,2,1,0:T(8,128)} %bitcast.107, f32[3,5,5,32,512]{4,3,2,1,0:T(8,128)} %all-gather.9.cloned.1.call-done), kind=kOutput, calls=%fused_computation.15 | convolution fusion | flops 3774873600 | bytes 13271040 | tf_op jit(solution)/shard_map/mstik,mctkj->mcsij/dot_general | solution.py:41
  388.0 0.0 copy-done.1
  388.0 2.6 fusion.16
  390.7 43.4 %reduce-scatter.5.cloned.1.call-done = f32[32,3,2,128]{3,0,2,1:T(8,128)} async-done(((f32[512,3,2,128]{3,0,2,1:T(8,128)}), f32[32,3,2,128]{3,0,2,1:T(8,128)}) %reduce-scatter.5.cloned.1.call-update) | async-done | bytes 98320 | tf_op jit(solution)/shard_map/reduce_scatter | solution.py:51
  434.1 2.4 fusion.28
  436.5 39.2 %all-gather.17.cloned.1.call-done = f32[6,6,32,512]{3,2,1,0:T(8,128)} async-done(((f32[6,6,32,128]{3,2,1,0:T(8,128)}), f32[6,6,32,512]{3,2,1,0:T(8,128)}) %all-gather.17.cloned.1.call-update) | async-done | bytes 2359312 | tf_op jit(solution)/shard_map/all_gather | solution.py:17
  475.7 3.4 convolution_bitcast_fusion
  479.0 0.0 copy-start.8
  479.1 2.1 copy.29
  481.2 0.0 copy-start.5
  481.2 0.0 all-reduce.3.cloned.1.call-update
  481.2 0.0 copy-done.8
  481.3 0.6 dynamic-slice
  482.5 0.9 maximum_negate_fusion
  483.4 112.9 %all-reduce.3.cloned.1.call-done = f32[512,3,2,128]{3,2,1,0:T(2,128)} async-done(((f32[512,3,2,128]{3,2,1,0:T(2,128)}), f32[512,3,2,128]{3,2,1,0:T(2,128)}) %all-reduce.3.cloned.1.call-update) | async-done | bytes 1572880
  596.3 0.9 constant_dynamic-slice_fusion
  597.3 0.0 copy-done.5
  597.3 0.7 bitcast_subtract_fusion
  (3 shorter events, 0.1 us)
Async XLA Ops:
  7.2 1.6 copy-start.7
  7.2 101.0 %all-gather.7.cloned.1.call-start = ((), (), s32[]{:S(2)}) async-start(), calls=%async_computation.2 | async-start | bytes 11796480 | tf_op jit(solution)/shard_map/all_gather | solution.py:19
  7.9 106.3 %copy-start.3 = (f32[3,5,32,128]{3,2,1,0:T(8,128)S(1)}, f32[3,5,32,128]{3,2,1,0:T(8,128)}, u32[]{:S(2)}) copy-start(f32[3,5,32,128]{3,2,1,0:T(8,128)} %param.8) | copy-start | bytes 737284
  7.9 145.6 %all-gather.11.cloned.1.call-start = ((), (), s32[]{:S(2)}) async-start(), calls=%async_computation.4 | async-start | bytes 4177920 | tf_op jit(solution)/shard_map/all_gather | solution.py:14
  8.7 204.4 %all-gather.9.cloned.1.call-start = ((), (), s32[]{:S(2)}) async-start(), calls=%async_computation.3 | async-start | bytes 6144000 | tf_op jit(solution)/shard_map/all_gather | solution.py:21
  114.1 166.6 %reduce-scatter.3.cloned.1.call-start = ((), (), s32[]{:S(2)}) async-start(), calls=%async_computation.5 | async-start | bytes 835584 | tf_op jit(solution)/shard_map/reduce_scatter | solution.py:24
  221.1 96.9 %copy-start.2 = (f32[3,5,32,128]{3,2,1,0:T(8,128)}, f32[3,5,32,128]{3,2,1,0:T(8,128)S(1)}, u32[]{:S(2)}) copy-start(f32[3,5,32,128]{3,2,1,0:T(8,128)S(1)} %fusion.22) | copy-start | bytes 737284
  221.1 59.6 %copy-start.6 = (f32[3,32,128]{2,1,0:T(8,128)S(1)}, f32[3,32,128]{2,1,0:T(8,128)}, u32[]{:S(2)}) copy-start(f32[3,32,128]{2,1,0:T(8,128)} %param.9) | copy-start | bytes 147460
  221.1 91.8 %copy-start = (f32[6,6,32,128]{3,2,1,0:T(8,128)S(1)}, f32[6,6,32,128]{3,2,1,0:T(8,128)}, u32[]{:S(2)}) copy-start(f32[6,6,32,128]{3,2,1,0:T(8,128)} %param.10) | copy-start | bytes 1769476
  224.7 88.2 %all-gather.15.cloned.1.call-start = ((), (), s32[]{:S(2)}) async-start(), calls=%async_computation.7 | async-start | bytes 1474560 | tf_op jit(solution)/shard_map/all_gather | solution.py:32
  281.5 36.4 %copy-start.4 = (f32[3,32,128]{2,1,0:T(8,128)}, f32[3,32,128]{2,1,0:T(8,128)S(1)}, u32[]{:S(2)}) copy-start(f32[3,32,128]{2,1,0:T(8,128)S(1)} %bitcast_subtract_fusion.1) | copy-start | bytes 147460
  282.3 95.6 %all-gather.13.cloned.1.call-start = ((), (), s32[]{:S(2)}) async-start(), calls=%async_computation.6 | async-start | bytes 10027008 | tf_op jit(solution)/shard_map/all_gather | solution.py:33
  282.9 151.2 %reduce-scatter.5.cloned.1.call-start = ((), (), s32[]{:S(2)}) async-start(), calls=%async_computation.8 | async-start | bytes 1671168 | tf_op jit(solution)/shard_map/reduce_scatter | solution.py:51
  318.0 157.7 %all-gather.17.cloned.1.call-start = ((), (), s32[]{:S(2)}) async-start(), calls=%async_computation.9 | async-start | bytes 2949120 | tf_op jit(solution)/shard_map/all_gather | solution.py:17
  318.8 277.6 %all-reduce.3.cloned.1.call-start = ((), (), s32[]{:S(2)}) async-start(), calls=%async_computation.10 | async-start | bytes 3145728
  377.9 10.1 %copy-start.1 = (f32[3,6,32,512]{3,2,1,0:T(8,128)S(1)}, f32[3,6,32,512]{3,2,1,0:T(8,128)}, u32[]{:S(2)}) copy-start(f32[3,6,32,512]{3,2,1,0:T(8,128)} %all-gather.15.cloned.1.call-done) | copy-start | bytes 3538948
  479.0 2.2 copy-start.8
  481.2 116.0 %copy-start.5 = (f32[6,32,128]{2,1,0:T(8,128)S(1)}, f32[6,32,128]{2,1,0:T(8,128)}, u32[]{:S(2)}) copy-start(f32[6,32,128]{2,1,0:T(8,128)} %param.11) | copy-start | bytes 294916
Sparse Core Ops, SparseCore 0:
  9.8 98.3 all-gather.6
  110.0 43.3 all-gather.10
  155.3 57.7 all-gather.8
  224.9 55.8 reduce-scatter.2
  283.1 29.7 all-gather.14
  314.8 63.1 all-gather.12
  380.6 53.3 reduce-scatter.4
  435.9 39.7 all-gather.16
  481.4 114.9 all-reduce.2
where the time goes:
time: 605 us; the launch traced here: 604 us
  waiting for transfers between devices  528 us (87%)
  matrix products  35.1 us (6%)
  between operations  14.7 us (2%)
  blocking collectives  13.2 us (2%)
  local copies, waits for them, and re-layouts  9.73 us (2%)
    unnamed x10, waiting for transfers between devices  116 us
    all_gather x1, waiting for transfers between devices, on_device(): ancestors = lax.all_gather(anc_inverse, 'leaf', axis=0, tiled=True)  99.3 us
    all_gather x1, waiting for transfers between devices, on_device(): stripes = lax.all_gather(selected, 'col', axis=4, tiled=True)  59.6 us
    all_gather x1, waiting for transfers between devices, on_device(): two_rows = lax.all_gather(lower_two, 'row', axis=2, tiled=True)  59 us
    reduce_scatter x1, waiting for transfers between devices, on_device(): lax.psum_scatter(jnp.einsum('mski,mskj->imj', cols_piece, offdiag_one, pr...  55.9 us
    reduce_scatter x1, waiting for transfers between devices, on_device(): lax.psum_scatter(jnp.einsum('mqki,mcqkj->imcj', stripe_piece, local_split...  43.4 us
    all_gather x1, waiting for transfers between devices, on_device(): lax.all_gather(lower_two, 'col', axis=3, tiled=True)  39.2 us
    all_gather x1, waiting for transfers between devices, on_device(): parent_stripe = lax.all_gather(parent_col, 'col', axis=3, tiled=True)  30 us
  transfers between devices with their start and end apart: 9, of which 9 were waited for; matrix products, arithmetic and copies ran while one was open for 5% of the time, Pallas kernels for 0%

commit v1 on v0

v1 whole, which is shorter than its diff:
```python
import jax
import jax.numpy as jnp
from jax import lax
from jax.experimental import pallas as pl
from jax.experimental.pallas import tpu as pltpu
from jax.sharding import PartitionSpec as P

F32 = jnp.float32
BF16 = jnp.bfloat16
MESH = pl.DeviceIdType.MESH
TR = 32
TC = 128
NM = 3
SK = 5
NC = 2
NJ = NM * NC
NL = NM * SK
NA2 = NJ * SK
NX = 4
NY = 4
NZ = 8
NR = 2 * NZ
LEAF_BLOCKS = 6
BLK = SK * SK
YH = 13
B1 = NL + NJ
XB1 = B1 + NM
GT = 5 * NM
GA = 8
N_COPIES = 4 + 4 + 4 * NM + 6 * NM + 2 * (8 + 8) + 1 + 8


def split(a):
    hi = a.astype(BF16)
    return hi, (a - hi.astype(F32)).astype(BF16)


def dot3(a, b, lhs_dim):
    ah, al = split(a)
    bh, bl = split(b)

    def one(u, v):
        return lax.dot_general(
            u, v, (((lhs_dim,), (0,)), ((), ())), preferred_element_type=F32
        )

    return one(ah, bh) + (one(ah, bl) + one(al, bh))


def kernel(
    st, g, low1, piv1, low2, piv2,
    off1, diag1, off2, diag2,
    xb1, xb2, x3, zb1, zb2, ysel, yo, yl, yr,
    zacc, pb, gp, sr, send_r, send_l, in_r, in_l,
    ssem, rsem,
):
    y = lax.axis_index("leaf")
    r = lax.axis_index("row")
    x = lax.axis_index("col")
    z = r // 2
    h = r % 2

    def wrap(v, n):
        return lax.rem(v + n, n)

    def dev(yy, rr, xx):
        return (yy, rr, xx)

    def zrow(zz):
        return 2 * wrap(zz, NZ) + h

    x_right, x_left = dev(y, r, wrap(x + 1, NX)), dev(y, r, wrap(x - 1, NX))
    y_right, y_left = dev(wrap(y + 1, NY), r, x), dev(wrap(y - 1, NY), r, x)
    z_right, z_left = dev(y, zrow(z + 1), x), dev(y, zrow(z - 1), x)
    sibling = dev(y, 2 * z + 1 - h, x)

    copies = []

    def send(src, dst, to):
        k = len(copies)
        c = pltpu.make_async_remote_copy(
            src_ref=src, dst_ref=dst, send_sem=ssem.at[k], recv_sem=rsem.at[k],
            device_id=to, device_id_type=MESH,
        )
        c.start()
        copies.append(c)
        return c

    barrier = pltpu.get_barrier_semaphore()
    partners = (x_right, x_left, y_right, y_left, z_right, z_left, sibling)
    for d in partners:
        pl.semaphore_signal(barrier, inc=1, device_id=d, device_id_type=MESH)
    pl.semaphore_wait(barrier, len(partners))

    def x_first(buf):
        own = buf.at[x]
        return send(own, own, x_right), send(own, own, x_left)

    def x_second(buf, first, n):
        half = n // 2
        first[0].wait_recv()
        a = buf.at[wrap(x - 1, NX), pl.ds(0, half)]
        fa = send(a, a, x_right)
        first[1].wait_recv()
        b = buf.at[wrap(x + 1, NX), pl.ds(half, n - half)]
        return fa, send(b, b, x_left)

    def z_start(buf):
        own = buf.at[r]
        return dict(
            buf=buf,
            right=send(own, own, z_right),
            left=send(own, own, z_left),
            sib=[send(own, own, sibling)],
        )

    def z_step(s, step, n):
        half = n // 2
        buf = s["buf"]
        last = step == 3
        right, left = s["right"], s["left"]
        right.wait_recv()
        a = buf.at[zrow(z - step)]
        ap = buf.at[zrow(z - step), pl.ds(0, half)] if last else a
        s["right"] = send(ap, ap, z_right)
        s["sib"].append(send(a, a, sibling))
        left.wait_recv()
        b = buf.at[zrow(z + step)]
        bp = buf.at[zrow(z + step), pl.ds(half, n - half)] if last else b
        s["left"] = send(bp, bp, z_left)
        s["sib"].append(send(b, b, sibling))

    def z_finish(s):
        s["right"].wait_recv()
        s["left"].wait_recv()
        far = s["buf"].at[zrow(z + 4)]
        s["sib"].append(send(far, far, sibling))
        for c in s["sib"]:
            c.wait_recv()

    xb1[x, 0:NL] = low1[...].reshape(NL, TR, TC)
    zb1[r, 0:NL] = low1[...].reshape(NL, TR, TC)
    for j in range(NJ):
        xb1[x, NL + j] = low2[j, SK]
        zb1[r, NL + j] = low2[j, SK]
    xb1[x, B1:XB1] = piv1[...]
    z1 = z_start(zb1)
    xf1 = x_first(xb1)

    def select(delta, m):
        base = (wrap(y + delta, NY) * NM + m) * SK

        def row(q, carry):
            sq = st[base + q]
            for p in range(SK):
                sp = st[base + p]
                mine = sp // LEAF_BLOCKS == y
                a = jnp.clip(sp - y * LEAF_BLOCKS, 0, LEAF_BLOCKS - 1)
                tile = g[a, sq]
                ysel[delta, m, q * SK + p] = jnp.where(mine, tile, jnp.zeros_like(tile))
            return carry

        lax.fori_loop(0, SK, row, 0)

    lo, hi = pl.ds(0, YH), pl.ds(YH, BLK - YH)
    opp = []
    for m in range(NM):
        select(2, m)
        opp.append(
            (
                send(ysel.at[2, m, lo], yo.at[m, lo], y_right),
                send(ysel.at[2, m, hi], yo.at[m, hi], y_left),
            )
        )
    direct = []
    for m in range(NM):
        select(1, m)
        c = send(ysel.at[1, m, hi], yl.at[m, hi], y_right)
        select(3, m)
        direct.append((c, send(ysel.at[3, m, lo], yr.at[m, lo], y_left)))

    merged = []

    def merge(m):
        opp[m][0].wait_recv()
        ysel[1, m, 0:YH] = ysel[1, m, 0:YH] + yo[m, 0:YH]
        c = send(ysel.at[1, m, lo], yl.at[m, lo], y_right)
        opp[m][1].wait_recv()
        ysel[3, m, YH:BLK] = ysel[3, m, YH:BLK] + yo[m, YH:BLK]
        merged.append((c, send(ysel.at[3, m, hi], yr.at[m, hi], y_left)))

    z_step(z1, 1, B1)
    for m in range(NM):
        select(0, m)
    merge(0)
    xs1 = x_second(xb1, xf1, XB1)
    z_step(z1, 2, B1)
    merge(1)
    z_step(z1, 3, B1)
    merge(2)
    for c in xs1:
        c.wait_recv()
    z_finish(z1)

    def stack(buf, first, count):
        return jnp.concatenate(
            [
                buf[c, pl.ds(first, count)].reshape(count * TR, TC)
                for c in range(NX)
            ],
            axis=1,
        )

    def rows_of(buf, i):
        return buf[:, i].reshape(NR * TR, TC)

    def correct(m, carry):
        lhs = jnp.concatenate([stack(xb1, m * SK, SK), stack(xb1, B1 + m, 1)], axis=0)
        rhs = jnp.concatenate(
            [rows_of(zb1, NL + m * NC + c) for c in range(NC)], axis=1
        )
        prod = dot3(lhs, rhs, 1)
        for c in range(NC):
            j = m * NC + c
            part = prod[:, c * TC : (c + 1) * TC]
            fixed = low2[j, 0:SK] - part[: SK * TR].reshape(SK, TR, TC)
            xb2[x, pl.ds(j * SK, SK)] = fixed
            zb2[r, pl.ds(j * SK, SK)] = fixed
            pb[j] = part[SK * TR :]
        return carry

    lax.fori_loop(0, NM, correct, 0)
    z2 = z_start(zb2)
    xf2 = x_first(xb2)

    xf3, xs3 = [], []

    def own_stripe(m):
        for c in direct[m] + merged[m]:
            c.wait_recv()
        x3[x, m] = ysel[0, m] + yl[m] + yr[m]
        own = x3.at[x, m]
        xf3.append((send(own, own, x_right), send(own, own, x_left)))

    def pass_stripe(m):
        half = YH
        xf3[m][0].wait_recv()
        a = x3.at[wrap(x - 1, NX), m, pl.ds(0, half)]
        fa = send(a, a, x_right)
        xf3[m][1].wait_recv()
        b = x3.at[wrap(x + 1, NX), m, pl.ds(half, BLK - half)]
        xs3.append((fa, send(b, b, x_left)))

    own_stripe(0)
    own_stripe(1)
    xs2 = x_second(xb2, xf2, NA2)
    z_step(z2, 1, NA2)
    own_stripe(2)
    pass_stripe(0)
    z_step(z2, 2, NA2)
    pass_stripe(1)
    z_step(z2, 3, NA2)
    pass_stripe(2)
    for c in xs2:
        c.wait_recv()
    z_finish(z2)

    for m in range(NM):
        for c in xs3[m]:
            c.wait_recv()
        zacc[...] = jnp.zeros_like(zacc)

        def block(q, carry, m=m):
            lhs = jnp.concatenate(
                [
                    x3[c, m, pl.ds(q * SK, SK)].reshape(SK * TR, TC)
                    for c in range(NX)
                ],
                axis=1,
            )
            rhs = jnp.concatenate(
                [rows_of(zb1, m * SK + q)]
                + [rows_of(zb2, (m * NC + c) * SK + q) for c in range(NC)],
                axis=1,
            )
            zacc[...] += dot3(lhs, rhs, 1)
            return carry

        lax.fori_loop(0, SK, block, 0)
        off1[m] = -zacc[:, 0:TC].reshape(SK, TR, TC)
        for c in range(NC):
            off2[m * NC + c, 0:SK] = -zacc[:, (c + 1) * TC : (c + 2) * TC].reshape(
                SK, TR, TC
            )
        left = dot3(stack(xb1, m * SK, SK), zacc[...], 0)
        parts = [left[:, b * TC : (b + 1) * TC] for b in range(1 + NC)]
        for c in range(NC):
            j = m * NC + c
            lhs = jnp.concatenate(
                [stack(xb2, j * SK, SK), stack(xb1, NL + j, 1)], axis=0
            )
            rhs = jnp.concatenate(
                [zacc[:, (c + 1) * TC : (c + 2) * TC], pb[j]], axis=0
            )
            parts.append(dot3(lhs, rhs, 0))
        for b in range(5):
            tiles = parts[b].reshape(NZ, 2, TR, TC)
            for hh in range(2):
                gp[hh, :, m * 5 + b] = tiles[:, hh]

    cs = send(gp.at[1 - h], sr, sibling)
    cs.wait_recv()

    def mine(zz, a, b):
        zz = wrap(zz, NZ)
        return gp[h, zz, a:b] + sr[zz, a:b]

    send_r[0, 0:GA] = mine(z + 4, 0, GA)
    a = pl.ds(0, GA)
    cr = send(send_r.at[0, a], in_r.at[0, a], z_right)
    send_l[0, GA:GT] = mine(z - 4, GA, GT)
    b = pl.ds(GA, GT - GA)
    cl = send(send_l.at[0, b], in_l.at[0, b], z_left)
    for s in range(1, 4):
        cr.wait_recv()
        if s == 1:
            send_r[1, 0:GA] = in_r[0, 0:GA] + mine(z + 3, 0, GA)
            send_r[1, GA:GT] = mine(z + 3, GA, GT)
        else:
            send_r[s] = in_r[s - 1] + mine(z + 4 - s, 0, GT)
        cr = send(send_r.at[s], in_r.at[s], z_right)
        cl.wait_recv()
        if s == 1:
            send_l[1, 0:GA] = mine(z - 3, 0, GA)
            send_l[1, GA:GT] = in_l[0, GA:GT] + mine(z - 3, GA, GT)
        else:
            send_l[s] = in_l[s - 1] + mine(z - 4 + s, 0, GT)
        cl = send(send_l.at[s], in_l.at[s], z_left)
    cr.wait_recv()
    cl.wait_recv()
    total = in_r[3] + in_l[3] + mine(z, 0, GT)
    for m in range(NM):
        diag1[m] = piv1[m] + total[m * 5]
        for c in range(NC):
            j = m * NC + c
            off2[j, SK] = total[m * 5 + 1 + c] - pb[j]
            diag2[j] = piv2[j] + total[m * 5 + 3 + c]
    assert len(copies) == N_COPIES, len(copies)
    for c in copies:
        c.wait_send()


def on_device(anc_inverse, struct_one, lower_one, pivot_inv_one, lower_two, pivot_inv_two):
    listed = lax.all_gather(struct_one, "leaf", axis=0, tiled=True).reshape(-1)
    tile = (TR, TC)

    def like(*lead):
        return jax.ShapeDtypeStruct(lead + tile, F32)

    def vmem(*lead):
        return pltpu.VMEM(lead + tile, F32)

    whole = pl.BlockSpec(memory_space=pltpu.VMEM)
    return pl.pallas_call(
        kernel,
        out_shape=(like(NM, SK), like(NM), like(NJ, SK + 1), like(NJ)),
        in_specs=[pl.BlockSpec(memory_space=pltpu.SMEM)] + [whole] * 5,
        out_specs=(whole,) * 4,
        scratch_shapes=[
            vmem(NX, XB1),
            vmem(NX, NA2),
            vmem(NX, NM, BLK),
            vmem(NR, B1),
            vmem(NR, NA2),
            vmem(NY, NM, BLK),
            vmem(NM, BLK),
            vmem(NM, BLK),
            vmem(NM, BLK),
            pltpu.VMEM((SK * TR, (1 + NC) * TC), F32),
            vmem(NJ),
            vmem(2, NZ, GT),
            vmem(NZ, GT),
            vmem(4, GT),
            vmem(4, GT),
            vmem(4, GT),
            vmem(4, GT),
            pltpu.SemaphoreType.DMA((N_COPIES,)),
            pltpu.SemaphoreType.DMA((N_COPIES,)),
        ],
        compiler_params=pltpu.CompilerParams(
            collective_id=0, has_side_effects=True, vmem_limit_bytes=60 * 2**20
        ),
    )(listed, anc_inverse, lower_one, pivot_inv_one, lower_two, pivot_inv_two)


def solution(mesh):
    placed = (
        P("leaf", None, "row", "col"),
        P("leaf", None),
        P("leaf", None, "row", "col"),
        P("leaf", "row", "col"),
        P("leaf", None, "row", "col"),
        P("leaf", "row", "col"),
    )
    return jax.shard_map(
        on_device,
        mesh=mesh,
        in_specs=placed,
        out_specs=(
            P("leaf", None, "row", "col"),
            P("leaf", "row", "col"),
            P("leaf", None, "row", "col"),
            P("leaf", "row", "col"),
        ),
        check_vma=False,
    )
```

time: 605 us -> 152 us (0.25)
  waiting for transfers between devices: 528 us -> 0 us
  Pallas kernels: 0 us -> 132 us
  matrix products: 35.1 us -> 0 us
  between operations: 14.7 us -> 0.64 us
    all_gather x6 -> x0, waiting for transfers between devices: 313 us -> none  [the longest x1 99.3 us: on_device(): ancestors = lax.all_gather(anc_inverse, 'leaf', axis=0, tiled=True)]
    pallas_call x0 -> x1, Pallas kernels: none -> 132 us  [on_device(): pl.pallas_call(kernel, out_shape=(like(NM, SK), like(NM), like(NJ, SK + 1...]
    unnamed x10 -> x0, waiting for transfers between devices: 116 us -> none
    reduce_scatter x2 -> x0, waiting for transfers between devices: 99.4 us -> none  [the longest x1 55.9 us: on_device(): lax.psum_scatter(jnp.einsum('mski,mskj->imj', cols_piece, offdiag_one, pr...]
    dot_general x7 -> x0, matrix products: 35.1 us -> none  [the longest x1 10.1 us: on_device(): jnp.einsum('mstik,mctkj->mcsij', stripes, rows_split[:, :, :struct_len],...]
  transfers between devices with their start and end apart: 9 -> 0, of which waited for: 9 -> 0; matrix products, arithmetic and copies ran while one was open for 5% -> 0% of each run, Pallas kernels for 0% -> 0%
where the time goes in v1:
time: 152 us; the launch traced here: 149 us
  Pallas kernels  132 us (87%)
  blocking collectives  9.56 us (6%)
  local copies, waits for them, and re-layouts  7.15 us (5%)
    pallas_call x1, Pallas kernels, on_device(): pl.pallas_call(kernel, out_shape=(like(NM, SK), like(NM), like(NJ, SK + 1...  132 us
    all_gather x1, blocking collectives, on_device(): listed = lax.all_gather(struct_one, 'leaf', axis=0, tiled=True).reshape(-1)  9.56 us
    unnamed x4, local copies, waits for them, and re-layouts  6.55 us

profile of v1, /device:TPU:1, one launch (start us, length us, event | category | flops | bytes accessed | tf_op | source)
XLA Modules:
  0.0 149.0 jit_solution(4021819406058908220)
XLA Ops:
  0.6 9.6 %all-gather = s32[4,3,5]{2,1,0:T(4,128)S(1)} all-gather(s32[1,3,5]{2,1,0:T(4,128)} %bitcast.1), channel_id=1, replica_groups=mesh['leaf'=4,'row'=16,'col'=4] {'leaf'}, dimensions={0}, use_global_device_ids=true | all-gather | bytes 300 | tf_op jit(solution)/shard_map/all_gather | solution.py:354
  10.2 0.6 reshape.11.st
  10.8 131.6 %shard_map.93 = (f32[3,5,32,128]{3,2,1,0:T(8,128)}, f32[3,32,128]{2,1,0:T(8,128)}, f32[6,6,32,128]{3,2,1,0:T(8,128)}, f32[6,32,128]{2,1,0:T(8,128)}) custom-call(s32[60]{0:T(128)} %reshape.11.st, f32[6,24,32,128]{3,2,1,0:T(8,128)} %g.1, f32[3,5,32,128]{3,2,1,0:T(8,128)} %low1.1, f32[3,32,128]{2,1,0:T(8,128)} %piv1.1, f32[6,6,32,128]{3,2,1,0:T(8,128)} %low2.1, ...), custom_call_target="tpu_custom_call" | custom-call | tf_op jit(solution)/shard_map/pallas_call | solution.py:364
  142.4 1.7 %copy.14 = f32[3,5,32,128]{3,2,1,0:T(8,128)} copy(f32[3,5,32,128]{3,2,1,0:T(8,128)} %get-tuple-element.8) | data formatting | bytes 491520
  144.1 1.4 copy.15
  145.5 1.9 %copy.16 = f32[6,6,32,128]{3,2,1,0:T(8,128)} copy(f32[6,6,32,128]{3,2,1,0:T(8,128)} %get-tuple-element.10) | data formatting | bytes 1179648
  147.4 1.5 %copy.17 = f32[6,32,128]{2,1,0:T(8,128)} copy(f32[6,32,128]{2,1,0:T(8,128)} %get-tuple-element.11) | data formatting | bytes 196608

commit v2 on v0

v2 whole, which is shorter than its diff:
```python
import jax
import jax.numpy as jnp
from jax import lax
from jax.experimental import pallas as pl
from jax.experimental.pallas import tpu as pltpu
from jax.sharding import PartitionSpec as P

F32 = jnp.float32
BF16 = jnp.bfloat16
I32 = jnp.int32
MESH = pl.DeviceIdType.MESH
TR = 32
TC = 128
NM = 3
SK = 5
NC = 2
NJ = NM * NC
NL = NM * SK
NX = 4
NY = 4
NZ = 8
NR = 2 * NZ
NA_LEAF = 6
NA_ALL = 24
BLK = SK * SK
UNITS = ((0, 13), (13, 12))
HALF = (7, 6)
GT = 3
N_OUT = 42
N_IN = 220
N_LOADS = 8
N_STORES = NM + NJ + 3


def split(a):
    hi = a.astype(BF16)
    return hi, (a - hi.astype(F32)).astype(BF16)


def dot3(a, b, lhs_dim):
    ah, al = split(a)
    bh, bl = split(b)

    def one(u, v):
        return lax.dot_general(
            u, v, (((lhs_dim,), (0,)), ((), ())), preferred_element_type=F32
        )

    return one(ah, bh) + (one(ah, bl) + one(al, bh))


def kernel(
    st, g_in, low1, piv1, low2, piv2,
    off1_out, diag1_out, off2_out, diag2_out,
    off1, diag1, off2, diag2,
    gv, av, p2, sv, xl, xb, xa, x3, zb, zl, za, ysel, yo, yn,
    zacc0, zacc1, pb, gp, sr, send_r, send_l, in_r, in_l,
    sm, ssem, rsem, lsem, msem, osem,
):
    y = lax.axis_index("leaf")
    r = lax.axis_index("row")
    x = lax.axis_index("col")
    z = r // 2
    h = r % 2

    def wrap(v, n):
        return lax.rem(v + n, n)

    def zrow(zz):
        return 2 * wrap(zz, NZ) + h

    x_right, x_left = (y, r, wrap(x + 1, NX)), (y, r, wrap(x - 1, NX))
    y_right, y_left = (wrap(y + 1, NY), r, x), (wrap(y - 1, NY), r, x)
    y_far = (wrap(y + 2, NY), r, x)
    z_right, z_left = (y, zrow(z + 1), x), (y, zrow(z - 1), x)
    sibling = (y, 2 * z + 1 - h, x)

    outs, ins, drains = [], [], []

    def next_out(sent):
        sem = ssem.at[len(outs)]
        outs.append(sem)
        drains.append((sent, sem))
        return sem

    def next_in():
        sem = rsem.at[len(ins)]
        ins.append(sem)
        return sem

    def take(ref, sem):
        pltpu.make_async_copy(ref, ref, sem).wait()

    def send(src, dst, to, out, into):
        c = pltpu.make_async_remote_copy(
            src_ref=src, dst_ref=dst, send_sem=out, recv_sem=into,
            device_id=to, device_id_type=MESH,
        )
        c.start()
        return c

    loads = [
        (low2.at[:, SK], zb.at[r]),
        (low1, xl.at[x, pl.ds(0, NL)]),
        (piv1, xl.at[x, pl.ds(NL, NM)]),
        (low1, zl.at[r]),
        (low2.at[:, SK], xb.at[x]),
        (g_in, gv),
        (low2.at[:, pl.ds(0, SK)], av),
        (piv2, p2),
    ]
    loads = [pltpu.make_async_copy(a, b, lsem.at[i]) for i, (a, b) in enumerate(loads)]
    for c in loads:
        c.start()
    lane = lax.broadcasted_iota(I32, (8, TC), 1)
    listed = jnp.zeros((8, TC), I32)
    for m in range(NM):
        for p in range(SK):
            listed = jnp.where(lane == m * SK + p, st[m, p], listed)
    sv[y] = listed

    barrier = pltpu.get_barrier_semaphore()
    partners = (x_right, x_left, y_right, y_left, y_far, z_right, z_left, sibling)
    for d in partners:
        pl.semaphore_signal(barrier, inc=1, device_id=d, device_id_type=MESH)
    pl.semaphore_wait(barrier, len(partners))

    class XRing:
        def __init__(self, at, n, half):
            self.at, self.n, self.half = at, n, half

        def start(self):
            self.out = next_out(self.at(pl.ds(0, 3)))
            own = self.at(x)
            self.a = send(own, own, x_right, self.out, next_in())
            self.b = send(own, own, x_left, self.out, next_in())

        def second(self):
            self.a.wait_recv()
            a = self.at(wrap(x - 1, NX)).at[pl.ds(0, self.half)]
            self.a = send(a, a, x_right, self.out, next_in())
            self.b.wait_recv()
            b = self.at(wrap(x + 1, NX)).at[pl.ds(self.half, self.n - self.half)]
            self.b = send(b, b, x_left, self.out, next_in())

        def finish(self):
            self.a.wait_recv()
            self.b.wait_recv()

    class ZRing:
        def __init__(self, at, n, half):
            self.at, self.n, self.half = at, n, half

        def start(self):
            self.out = next_out(self.at(pl.ds(0, 2 * NZ - 1)))
            self.sib = next_in()
            own = self.at(r)
            self.a = send(own, own, z_right, self.out, next_in())
            self.b = send(own, own, z_left, self.out, next_in())
            send(own, own, sibling, self.out, self.sib)

        def step(self, i):
            self.a.wait_recv()
            a = self.at(zrow(z - i))
            part = a.at[pl.ds(0, self.half)] if i == 3 else a
            self.a = send(part, part, z_right, self.out, next_in())
            self.b.wait_recv()
            b = self.at(zrow(z + i))
            part = b.at[pl.ds(self.half, self.n - self.half)] if i == 3 else b
            self.b = send(part, part, z_left, self.out, next_in())
            send(a, a, sibling, self.out, self.sib)
            send(b, b, sibling, self.out, self.sib)

        def last(self):
            self.a.wait_recv()
            self.b.wait_recv()
            far = self.at(zrow(z + 4))
            send(far, far, sibling, self.out, self.sib)

        def finish(self):
            take(self.at(pl.ds(0, NZ)), self.sib)

    z_b = [
        ZRing(lambda i, m=m: zb.at[i, pl.ds(m * NC, NC)], NC, 1) for m in range(NM)
    ]
    z_l = [
        ZRing(lambda i, m=m: zl.at[i, pl.ds(m * SK, SK)], SK, 2 + m % 2)
        for m in range(NM)
    ]
    z_a = [ZRing(lambda i, j=j: za.at[i, j], SK, 2 + j % 2) for j in range(NJ)]
    x_lp = XRing(lambda i: xl.at[i], NL + NM, (NL + NM) // 2)
    x_b = XRing(lambda i: xb.at[i], NJ, NJ // 2)
    x_a = [XRing(lambda i, m=m: xa.at[i, m], NC * SK, SK) for m in range(NM)]
    x_s = [
        XRing(lambda i, k=k: x3.at[i, k // 2, pl.ds(*UNITS[k % 2])], UNITS[k % 2][1], HALF[k % 2])
        for k in range(2 * NM)
    ]

    listed_in = next_in()

    def send_lists():
        out = next_out(sv.at[pl.ds(0, NY - 1)])
        own = sv.at[y]
        for d in (y_right, y_left, y_far):
            send(own, own, d, out, listed_in)

    def take_lists():
        take(sv.at[pl.ds(0, NY - 1)], listed_in)
        to_scalars = pltpu.make_async_copy(sv, sm, msem)
        to_scalars.start()
        to_scalars.wait()

    def select(delta, k):
        m, (first, count) = k // 2, UNITS[k % 2]
        to = wrap(y + delta, NY)

        def tile_of(e, carry):
            sq = sm[to, 0, m * SK + e // SK]
            sp = sm[to, 0, m * SK + lax.rem(e, SK)]
            mine = sp // NA_LEAF == y
            a = jnp.clip(sp - y * NA_LEAF, 0, NA_LEAF - 1)
            tile = gv[a, sq]
            ysel[delta, m, e] = jnp.where(mine, tile, jnp.zeros_like(tile))
            return carry

        lax.fori_loop(first, first + count, tile_of, 0)

    def halves(k):
        first, count = UNITS[k % 2]
        half = HALF[k % 2]
        return pl.ds(first, half), pl.ds(first + half, count - half)

    y_out = [next_out(ysel.at[pl.ds(0, 3), 0, pl.ds(0, n)]) for _, n in UNITS * NM]
    far_in = [next_in() for _ in range(2 * NM)]
    near_in = [next_in() for _ in range(2 * NM)]

    def y_far_half(k):
        select(2, k)
        m, (lo, hi) = k // 2, halves(k)
        send(ysel.at[2, m, lo], yo.at[m, lo], y_right, y_out[k], far_in[k])
        send(ysel.at[2, m, hi], yo.at[m, hi], y_left, y_out[k], far_in[k])

    def y_near_half(k):
        m, (lo, hi) = k // 2, halves(k)
        select(1, k)
        send(ysel.at[1, m, hi], yn.at[m, 0, hi], y_right, y_out[k], near_in[k])
        select(3, k)
        send(ysel.at[3, m, lo], yn.at[m, 1, lo], y_left, y_out[k], near_in[k])

    def y_merge(k):
        m, (lo, hi) = k // 2, halves(k)
        take(yo.at[m, pl.ds(*UNITS[k % 2])], far_in[k])
        ysel[1, m, lo] = ysel[1, m, lo] + yo[m, lo]
        send(ysel.at[1, m, lo], yn.at[m, 0, lo], y_right, y_out[k], near_in[k])
        ysel[3, m, hi] = ysel[3, m, hi] + yo[m, hi]
        send(ysel.at[3, m, hi], yn.at[m, 1, hi], y_left, y_out[k], near_in[k])

    def y_last(k):
        m, tiles = k // 2, pl.ds(*UNITS[k % 2])
        take(yn.at[m, :, tiles], near_in[k])
        x3[x, m, tiles] = ysel[0, m, tiles] + yn[m, 0, tiles] + yn[m, 1, tiles]
        x_s[k].start()

    def wide(tiles):
        return jnp.concatenate([t.reshape(-1, TC) for t in tiles], axis=1)

    def tall(tiles):
        return tiles.reshape(NR * TR, TC)

    stores = []

    def store(src, dst):
        c = pltpu.make_async_copy(src, dst, osem.at[len(stores)])
        c.start()
        stores.append(c)

    def low_cols(m):
        return wide([xl[i, m * SK : (m + 1) * SK] for i in range(NX)])

    def correct(m):
        lhs = jnp.concatenate(
            [low_cols(m), wide([xl[i, NL + m] for i in range(NX)])], axis=0
        )
        rhs = jnp.concatenate([tall(zb[:, m * NC + c]) for c in range(NC)], axis=1)
        prod = dot3(lhs, rhs, 1)
        for c in range(NC):
            j = m * NC + c
            part = prod[:, c * TC : (c + 1) * TC]
            fixed = av[j] - part[: SK * TR].reshape(SK, TR, TC)
            xa[x, m, c * SK : (c + 1) * SK] = fixed
            za[r, j] = fixed
            pb[j] = part[SK * TR :]

    def multiply(j):
        m, c = j // NC, j % NC
        zacc = zacc1 if c else zacc0
        zacc[...] = jnp.zeros_like(zacc)

        def block(q, carry):
            lhs = wide([x3[i, m, pl.ds(q * SK, SK)] for i in range(NX)])
            rhs = tall(za[:, j, q])
            if c == 0:
                rhs = jnp.concatenate([tall(zl[:, m * SK + q]), rhs], axis=1)
            zacc[...] += dot3(lhs, rhs, 1)
            return carry

        lax.fori_loop(0, SK, block, 0)
        own = zacc[:, (1 - c) * TC : (2 - c) * TC] if c == 0 else zacc[...]
        left = dot3(low_cols(m), zacc[...], 0)
        parts = [left[:, b * TC : (b + 1) * TC] for b in range(2 - c)]
        lhs = jnp.concatenate(
            [
                wide([xa[i, m, c * SK : (c + 1) * SK] for i in range(NX)]),
                wide([xb[i, j] for i in range(NX)]),
            ],
            axis=0,
        )
        parts.append(dot3(lhs, jnp.concatenate([own, pb[j]], axis=0), 0))
        for b, part in enumerate(parts):
            tiles = part.reshape(NZ, 2, TR, TC)
            for hh in range(2):
                gp[hh, j, :, b] = tiles[:, hh]
        reduces[j].share()
        off2[j, 0:SK] = -own.reshape(SK, TR, TC)
        upper = pl.ds(0, SK)
        store(off2.at[j, upper], off2_out.at[j, upper])
        if c == 0:
            off1[m] = -zacc[:, 0:TC].reshape(SK, TR, TC)
            store(off1.at[m], off1_out.at[m])

    class Reduce:
        def __init__(self, j):
            self.j, self.m, self.c = j, j // NC, j % NC
            self.n = 3 - self.c
            self.half = 1 if self.c or self.m % 2 else 2

        def mine(self, zz, a=0, b=None):
            zz = wrap(zz, NZ)
            b = self.n if b is None else b
            return gp[h, self.j, zz, a:b] + sr[self.j, zz, a:b]

        def share(self):
            part = pl.ds(0, self.n)
            out = next_out(gp.at[0, self.j, :, part])
            self.s = send(
                gp.at[1 - h, self.j, :, part],
                sr.at[self.j, :, part],
                sibling,
                out,
                next_in(),
            )

        def start(self):
            j, n, k = self.j, self.n, self.half
            self.out = next_out(gp.at[0, j, pl.ds(0, NZ - 1), pl.ds(0, n)])
            self.s.wait_recv()
            a, b = pl.ds(0, k), pl.ds(k, n - k)
            send_r[j, 0, 0:k] = self.mine(z + 4, 0, k)
            self.a = send(
                send_r.at[j, 0, a], in_r.at[j, 0, a], z_right, self.out, next_in()
            )
            send_l[j, 0, k:n] = self.mine(z - 4, k, n)
            self.b = send(
                send_l.at[j, 0, b], in_l.at[j, 0, b], z_left, self.out, next_in()
            )

        def step(self, s):
            j, n, k = self.j, self.n, self.half
            every = pl.ds(0, n)
            self.a.wait_recv()
            if s == 1:
                send_r[j, 1, 0:k] = in_r[j, 0, 0:k] + self.mine(z + 3, 0, k)
                send_r[j, 1, k:n] = self.mine(z + 3, k, n)
            else:
                send_r[j, s, 0:n] = in_r[j, s - 1, 0:n] + self.mine(z + 4 - s)
            self.a = send(
                send_r.at[j, s, every], in_r.at[j, s, every], z_right, self.out, next_in()
            )
            self.b.wait_recv()
            if s == 1:
                send_l[j, 1, 0:k] = self.mine(z - 3, 0, k)
                send_l[j, 1, k:n] = in_l[j, 0, k:n] + self.mine(z - 3, k, n)
            else:
                send_l[j, s, 0:n] = in_l[j, s - 1, 0:n] + self.mine(z - 4 + s)
            self.b = send(
                send_l.at[j, s, every], in_l.at[j, s, every], z_left, self.out, next_in()
            )

        def finish(self):
            j, m, c, n = self.j, self.m, self.c, self.n
            self.a.wait_recv()
            self.b.wait_recv()
            total = in_r[j, 3, 0:n] + in_l[j, 3, 0:n] + self.mine(z)
            if c == 0:
                diag1[m] = xl[x, NL + m] + total[0]
            off2[j, SK] = total[n - 2] - pb[j]
            diag2[j] = p2[j] + total[n - 1]

    reduces = [Reduce(j) for j in range(NJ)]

    for c in loads:
        c.wait()

    x_lp.start()
    z_b[0].start()
    send_lists()
    z_l[0].start()
    z_b[1].start()
    z_b[2].start()
    z_b[0].step(1)
    x_b.start()
    take_lists()
    y_far_half(0)
    select(0, 0)
    select(0, 3)
    y_near_half(0)
    z_b[1].step(1)
    z_b[2].step(1)
    z_b[0].step(2)
    select(0, 2)
    select(0, 5)
    z_l[0].step(1)
    select(0, 4)
    x_lp.second()
    z_b[1].step(2)
    y_merge(0)
    y_far_half(1)
    y_near_half(1)
    z_b[0].step(3)
    z_l[1].start()
    z_l[2].start()
    x_b.second()
    z_l[0].step(2)
    z_b[1].step(3)
    z_b[2].step(2)
    z_b[0].last()
    y_last(0)
    z_b[0].finish()
    z_l[1].step(1)
    x_lp.finish()
    x_b.finish()
    correct(0)
    z_a[0].start()
    z_a[1].start()
    y_merge(1)
    y_far_half(2)
    select(0, 1)
    y_near_half(2)
    x_a[0].start()
    z_l[0].step(3)
    z_b[1].last()
    z_b[2].step(3)
    z_b[1].finish()
    correct(1)
    x_a[1].start()
    z_a[3].start()
    z_l[1].step(2)
    y_last(1)
    x_s[0].second()
    z_a[2].start()
    z_l[2].step(1)
    z_a[0].step(1)
    y_merge(2)
    y_far_half(3)
    y_near_half(3)
    z_a[1].step(1)
    x_a[0].second()
    z_b[2].last()
    z_b[2].finish()
    correct(2)
    x_a[2].start()
    z_a[5].start()
    z_a[3].step(1)
    z_l[0].last()
    x_a[1].second()
    z_l[0].finish()
    z_l[1].step(3)
    y_last(2)
    z_a[4].start()
    z_a[2].step(1)
    y_merge(3)
    y_far_half(4)
    y_near_half(4)
    x_s[1].second()
    z_l[2].step(2)
    z_a[0].step(2)
    x_s[0].finish()
    z_a[1].step(2)
    x_a[0].finish()
    z_a[5].step(1)
    y_last(3)
    y_merge(4)
    y_far_half(5)
    y_near_half(5)
    z_a[3].step(2)
    z_l[1].last()
    x_a[2].second()
    x_a[1].finish()
    z_l[1].finish()
    z_a[4].step(1)
    y_last(4)
    z_l[2].step(3)
    y_merge(5)
    z_a[0].step(3)
    x_s[1].finish()
    z_a[1].step(3)
    y_last(5)
    z_a[5].step(2)
    z_a[3].step(3)
    z_a[4].step(2)
    z_a[2].step(2)
    z_l[2].last()
    z_a[0].last()
    x_a[2].finish()
    z_a[1].last()
    z_a[0].finish()
    multiply(0)
    z_a[1].finish()
    x_s[4].second()
    multiply(1)
    reduces[0].start()
    z_a[3].last()
    z_l[2].finish()
    x_s[2].second()
    z_a[4].step(3)
    z_a[3].finish()
    reduces[1].start()
    z_a[5].step(3)
    x_s[5].second()
    reduces[0].step(1)
    z_a[2].step(3)
    x_s[3].second()
    z_a[4].last()
    x_s[4].finish()
    z_a[5].last()
    z_a[4].finish()
    reduces[1].step(1)
    z_a[5].finish()
    reduces[0].step(2)
    x_s[2].finish()
    z_a[2].last()
    z_a[2].finish()
    reduces[1].step(2)
    x_s[5].finish()
    multiply(5)
    multiply(4)
    reduces[0].step(3)
    reduces[5].start()
    x_s[3].finish()
    multiply(2)
    reduces[4].start()
    reduces[1].step(3)
    multiply(3)
    reduces[2].start()
    reduces[0].finish()
    reduces[3].start()
    reduces[4].step(1)
    reduces[1].finish()
    reduces[5].step(1)
    reduces[2].step(1)
    reduces[3].step(1)
    reduces[4].step(2)
    reduces[5].step(2)
    reduces[2].step(2)
    reduces[3].step(2)
    reduces[4].step(3)
    reduces[5].step(3)
    reduces[2].step(3)
    reduces[3].step(3)
    reduces[4].finish()
    reduces[5].finish()
    reduces[2].finish()
    reduces[3].finish()

    last_row = pl.ds(SK, 1)
    store(off2.at[:, last_row], off2_out.at[:, last_row])
    store(diag1, diag1_out)
    store(diag2, diag2_out)
    for sent, sem in drains:
        take(sent, sem)
    for c in stores:
        c.wait()


def hand_over(*refs):
    n = len(refs) // 2
    for a, b in zip(refs[:n], refs[n:]):
        b[...] = a[...]


def on_device(anc_inverse, struct_one, lower_one, pivot_inv_one, lower_two, pivot_inv_two):
    tile = (TR, TC)

    def vmem(*lead):
        return pltpu.VMEM(lead + tile, F32)

    whole = pl.BlockSpec(memory_space=pltpu.VMEM)
    there = pl.BlockSpec(memory_space=pl.ANY)
    outs = tuple(
        jax.ShapeDtypeStruct(lead + tile, F32)
        for lead in ((NM, SK), (NM,), (NJ, SK + 1), (NJ,))
    )
    made = pl.pallas_call(
        kernel,
        out_shape=outs,
        in_specs=[pl.BlockSpec(memory_space=pltpu.SMEM)] + [there] * 5,
        out_specs=(there,) * 4,
        scratch_shapes=[
            vmem(NM, SK),
            vmem(NM),
            vmem(NJ, SK + 1),
            vmem(NJ),
            vmem(NA_LEAF, NA_ALL),
            vmem(NJ, SK),
            vmem(NJ),
            pltpu.VMEM((NY, 8, TC), I32),
            vmem(NX, NL + NM),
            vmem(NX, NJ),
            vmem(NX, NM, NC * SK),
            vmem(NX, NM, BLK),
            vmem(NR, NJ),
            vmem(NR, NL),
            vmem(NR, NJ, SK),
            vmem(NY, NM, BLK),
            vmem(NM, BLK),
            vmem(NM, 2, BLK),
            pltpu.VMEM((SK * TR, 2 * TC), F32),
            pltpu.VMEM((SK * TR, TC), F32),
            vmem(NJ),
            vmem(2, NJ, NZ, GT),
            vmem(NJ, NZ, GT),
            vmem(NJ, 4, GT),
            vmem(NJ, 4, GT),
            vmem(NJ, 4, GT),
            vmem(NJ, 4, GT),
            pltpu.SMEM((NY, 8, TC), I32),
            pltpu.SemaphoreType.DMA((N_OUT,)),
            pltpu.SemaphoreType.DMA((N_IN,)),
            pltpu.SemaphoreType.DMA((N_LOADS,)),
            pltpu.SemaphoreType.DMA,
            pltpu.SemaphoreType.DMA((N_STORES,)),
        ],
        compiler_params=pltpu.CompilerParams(
            collective_id=0, has_side_effects=True, vmem_limit_bytes=56 * 2**20
        ),
    )(
        struct_one,
        anc_inverse,
        lower_one.reshape(NL, TR, TC),
        pivot_inv_one,
        lower_two,
        pivot_inv_two,
    )
    return pl.pallas_call(
        hand_over,
        out_shape=outs,
        in_specs=[whole] * 4,
        out_specs=(whole,) * 4,
    )(*made)


def solution(mesh):
    placed = (
        P("leaf", None, "row", "col"),
        P("leaf", None),
        P("leaf", None, "row", "col"),
        P("leaf", "row", "col"),
        P("leaf", None, "row", "col"),
        P("leaf", "row", "col"),
    )
    return jax.shard_map(
        on_device,
        mesh=mesh,
        in_specs=placed,
        out_specs=(
            P("leaf", None, "row", "col"),
            P("leaf", "row", "col"),
            P("leaf", None, "row", "col"),
            P("leaf", "row", "col"),
        ),
        check_vma=False,
    )
```

time: 605 us -> 111 us (0.18)
  waiting for transfers between devices: 528 us -> 0 us
  Pallas kernels: 0 us -> 111 us
  matrix products: 35.1 us -> 0 us
  between operations: 14.7 us -> 0.64 us
  blocking collectives: 13.2 us -> 0 us
  local copies, waits for them, and re-layouts: 9.73 us -> 0 us
    all_gather x6 -> x0, waiting for transfers between devices: 313 us -> none  [the longest x1 99.3 us: on_device(): ancestors = lax.all_gather(anc_inverse, 'leaf', axis=0, tiled=True)]
    unnamed x10 -> x0, waiting for transfers between devices: 116 us -> none
    pallas_call x0 -> x2, Pallas kernels: none -> 111 us  [the longest x1 108 us: on_device(): pl.pallas_call(kernel, out_shape=outs, in_specs=[pl.BlockSpec(memory_spac...]
    reduce_scatter x2 -> x0, waiting for transfers between devices: 99.4 us -> none  [the longest x1 55.9 us: on_device(): lax.psum_scatter(jnp.einsum('mski,mskj->imj', cols_piece, offdiag_one, pr...]
    dot_general x7 -> x0, matrix products: 35.1 us -> none  [the longest x1 10.1 us: on_device(): jnp.einsum('mstik,mctkj->mcsij', stripes, rows_split[:, :, :struct_len],...]
    all_gather x1 -> x0, blocking collectives: 13.2 us -> none  [on_device(): lax.all_gather(lower_one, 'col', axis=3, tiled=True)]
  transfers between devices with their start and end apart: 9 -> 0, of which waited for: 9 -> 0; matrix products, arithmetic and copies ran while one was open for 5% -> 0% of each run, Pallas kernels for 0% -> 0%
where the time goes in v2:
time: 111 us
  Pallas kernels  111 us (100%)
    pallas_call x1, Pallas kernels, on_device(): pl.pallas_call(kernel, out_shape=outs, in_specs=[pl.BlockSpec(memory_spac...  108 us

profile of v2, /device:TPU:1, one launch (start us, length us, event | category | flops | bytes accessed | tf_op | source)
XLA Modules:
  0.0 111.2 jit_solution(12080631592518030429)
XLA Ops:
  0.6 108.4 %shard_map.93 = (f32[3,5,32,128]{3,2,1,0:T(8,128)}, f32[3,32,128]{2,1,0:T(8,128)}, f32[6,6,32,128]{3,2,1,0:T(8,128)}, f32[6,32,128]{2,1,0:T(8,128)}) custom-call(s32[3,5]{1,0:T(4,128)} %st.1, f32[6,24,32,128]{3,2,1,0:T(8,128)} %g_in.1, f32[15,32,128]{2,1,0:T(8,128)} %bitcast.1, f32[3,32,128]{2,1,0:T(8,128)} %piv1.1, f32[6,6,32,128]{3,2,1,0:T(8,128)} %low2.1, ...), custom_call_target="tpu_custom_call" | custom-call | tf_op jit(solution)/shard_map/pallas_call | solution.py:603
  109.1 2.2 %shard_map.94 = (f32[3,5,32,128]{3,2,1,0:T(8,128)}, f32[3,32,128]{2,1,0:T(8,128)}, f32[6,6,32,128]{3,2,1,0:T(8,128)}, f32[6,32,128]{2,1,0:T(8,128)}) custom-call(f32[3,5,32,128]{3,2,1,0:T(8,128)} %get-tuple-element.8.refs_0_, f32[3,32,128]{2,1,0:T(8,128)} %get-tuple-element.9.refs_1_, f32[6,6,32,128]{3,2,1,0:T(8,128)} %get-tuple-element.10.refs_2_, ...), custom_call_target="tpu_custom_call" | custom-call | tf_op jit(solution)/shard_map/pallas_call | solution.py:654

commit v3 on v2

--- a/solution.py
+++ b/solution.py
@@ -401,176 +401,176 @@
     for c in loads:
         c.wait()
 
+    send_lists()
+    z_b[0].start()
+    z_b[1].start()
     x_lp.start()
-    z_b[0].start()
-    send_lists()
+    z_b[2].start()
     z_l[0].start()
-    z_b[1].start()
-    z_b[2].start()
+    z_l[1].start()
+    z_l[2].start()
+    take_lists()
+    select(0, 4)
+    y_far_half(0)
+    select(0, 1)
     z_b[0].step(1)
+    y_near_half(0)
+    select(0, 2)
+    z_b[2].step(1)
+    select(0, 0)
+    select(0, 5)
+    select(0, 3)
+    z_b[1].step(1)
+    z_l[1].step(1)
     x_b.start()
-    take_lists()
-    y_far_half(0)
-    select(0, 0)
-    select(0, 3)
-    y_near_half(0)
-    z_b[1].step(1)
-    z_b[2].step(1)
-    z_b[0].step(2)
-    select(0, 2)
-    select(0, 5)
-    z_l[0].step(1)
-    select(0, 4)
-    x_lp.second()
-    z_b[1].step(2)
     y_merge(0)
     y_far_half(1)
+    z_b[0].step(2)
+    x_lp.second()
+    z_l[2].step(1)
     y_near_half(1)
+    z_b[1].step(2)
+    z_b[2].step(2)
+    x_b.second()
     z_b[0].step(3)
-    z_l[1].start()
-    z_l[2].start()
-    x_b.second()
-    z_l[0].step(2)
+    y_last(0)
+    z_l[2].step(2)
+    x_lp.finish()
+    z_b[2].step(3)
+    z_b[0].last()
+    z_l[0].step(1)
     z_b[1].step(3)
-    z_b[2].step(2)
-    z_b[0].last()
-    y_last(0)
     z_b[0].finish()
-    z_l[1].step(1)
-    x_lp.finish()
-    x_b.finish()
     correct(0)
+    x_a[0].start()
+    z_a[1].start()
     z_a[0].start()
-    z_a[1].start()
+    z_l[2].step(3)
+    z_b[2].last()
     y_merge(1)
     y_far_half(2)
-    select(0, 1)
     y_near_half(2)
-    x_a[0].start()
-    z_l[0].step(3)
+    x_s[0].second()
     z_b[1].last()
-    z_b[2].step(3)
-    z_b[1].finish()
-    correct(1)
-    x_a[1].start()
-    z_a[3].start()
-    z_l[1].step(2)
+    z_l[0].step(2)
+    z_b[2].finish()
+    correct(2)
+    z_a[4].start()
+    z_a[1].step(1)
+    x_a[2].start()
+    x_b.finish()
     y_last(1)
-    x_s[0].second()
-    z_a[2].start()
-    z_l[2].step(1)
     z_a[0].step(1)
+    x_a[0].second()
+    x_s[0].finish()
     y_merge(2)
     y_far_half(3)
     y_near_half(3)
-    z_a[1].step(1)
-    x_a[0].second()
-    z_b[2].last()
-    z_b[2].finish()
-    correct(2)
-    x_a[2].start()
-    z_a[5].start()
-    z_a[3].step(1)
+    z_l[0].step(3)
+    z_a[4].step(1)
+    x_a[2].second()
+    z_a[1].step(2)
+    z_a[0].step(2)
+    y_last(2)
+    x_s[1].second()
+    y_merge(3)
     z_l[0].last()
-    x_a[1].second()
+    z_a[4].step(2)
+    x_a[0].finish()
     z_l[0].finish()
-    z_l[1].step(3)
-    y_last(2)
-    z_a[4].start()
-    z_a[2].step(1)
-    y_merge(3)
     y_far_half(4)
     y_near_half(4)
-    x_s[1].second()
-    z_l[2].step(2)
-    z_a[0].step(2)
-    x_s[0].finish()
-    z_a[1].step(2)
-    x_a[0].finish()
-    z_a[5].step(1)
+    z_a[5].start()
+    z_a[1].step(3)
+    z_l[1].step(2)
+    z_a[0].step(3)
     y_last(3)
+    z_a[4].step(3)
+    z_l[2].last()
+    x_a[2].finish()
+    z_b[1].finish()
+    correct(1)
+    z_a[3].start()
+    z_a[2].start()
     y_merge(4)
     y_far_half(5)
+    x_s[2].second()
     y_near_half(5)
+    z_l[2].finish()
+    z_a[5].step(1)
+    x_s[1].finish()
+    z_l[1].step(3)
+    z_a[1].last()
+    x_a[1].start()
+    z_a[1].finish()
+    z_a[4].last()
+    z_a[0].last()
+    y_last(4)
+    z_a[0].finish()
+    x_s[3].second()
+    z_a[3].step(1)
+    multiply(0)
+    y_merge(5)
+    x_s[2].finish()
+    z_a[2].step(1)
+    reduces[0].start()
+    multiply(1)
+    z_l[1].last()
+    z_a[5].step(2)
+    z_a[4].finish()
+    z_l[1].finish()
+    reduces[1].start()
     z_a[3].step(2)
-    z_l[1].last()
-    x_a[2].second()
+    y_last(5)
+    reduces[0].step(1)
+    z_a[2].step(2)
+    x_a[1].second()
+    z_a[5].step(3)
+    x_s[4].second()
+    reduces[1].step(1)
+    x_s[3].finish()
+    z_a[3].step(3)
+    reduces[0].step(2)
+    z_a[2].step(3)
+    z_a[5].last()
+    reduces[1].step(2)
+    x_s[5].second()
+    z_a[3].last()
+    z_a[5].finish()
+    z_a[3].finish()
+    reduces[0].step(3)
+    z_a[2].last()
     x_a[1].finish()
-    z_l[1].finish()
-    z_a[4].step(1)
-    y_last(4)
-    z_l[2].step(3)
-    y_merge(5)
-    z_a[0].step(3)
-    x_s[1].finish()
-    z_a[1].step(3)
-    y_last(5)
-    z_a[5].step(2)
-    z_a[3].step(3)
-    z_a[4].step(2)
-    z_a[2].step(2)
-    z_l[2].last()
-    z_a[0].last()
-    x_a[2].finish()
-    z_a[1].last()
-    z_a[0].finish()
-    multiply(0)
-    z_a[1].finish()
-    x_s[4].second()
-    multiply(1)
-    reduces[0].start()
-    z_a[3].last()
-    z_l[2].finish()
-    x_s[2].second()
-    z_a[4].step(3)
-    z_a[3].finish()
-    reduces[1].start()
-    z_a[5].step(3)
-    x_s[5].second()
-    reduces[0].step(1)
-    z_a[2].step(3)
-    x_s[3].second()
-    z_a[4].last()
+    multiply(3)
+    z_a[2].finish()
     x_s[4].finish()
-    z_a[5].last()
-    z_a[4].finish()
-    reduces[1].step(1)
-    z_a[5].finish()
-    reduces[0].step(2)
-    x_s[2].finish()
-    z_a[2].last()
-    z_a[2].finish()
-    reduces[1].step(2)
+    multiply(2)
+    reduces[3].start()
+    reduces[1].step(3)
     x_s[5].finish()
-    multiply(5)
     multiply(4)
-    reduces[0].step(3)
-    reduces[5].start()
-    x_s[3].finish()
-    multiply(2)
-    reduces[4].start()
-    reduces[1].step(3)
-    multiply(3)
     reduces[2].start()
     reduces[0].finish()
-    reduces[3].start()
+    multiply(5)
+    reduces[4].start()
+    reduces[1].finish()
+    reduces[5].start()
+    reduces[3].step(1)
+    reduces[2].step(1)
     reduces[4].step(1)
-    reduces[1].finish()
     reduces[5].step(1)
-    reduces[2].step(1)
-    reduces[3].step(1)
+    reduces[3].step(2)
+    reduces[2].step(2)
     reduces[4].step(2)
     reduces[5].step(2)
-    reduces[2].step(2)
-    reduces[3].step(2)
+    reduces[3].step(3)
+    reduces[2].step(3)
     reduces[4].step(3)
     reduces[5].step(3)
-    reduces[2].step(3)
-    reduces[3].step(3)
+    reduces[3].finish()
+    reduces[2].finish()
     reduces[4].finish()
     reduces[5].finish()
-    reduces[2].finish()
-    reduces[3].finish()
 
     last_row = pl.ds(SK, 1)
     store(off2.at[:, last_row], off2_out.at[:, last_row])

time: 111 us -> 109 us (0.982)
  Pallas kernels: 111 us -> 108 us
    pallas_call x1, Pallas kernels: 108 us -> 106 us  [on_device(): pl.pallas_call(kernel, out_shape=outs, in_specs=[pl.BlockSpec(memory_spac...]
where the time goes in v3:
time: 109 us
  Pallas kernels  108 us (99%)
    pallas_call x1, Pallas kernels, on_device(): pl.pallas_call(kernel, out_shape=outs, in_specs=[pl.BlockSpec(memory_spac...  106 us

profile of v3, /device:TPU:1, one launch (start us, length us, event | category | flops | bytes accessed | tf_op | source)
XLA Modules:
  0.0 108.8 jit_solution(5061846087088718700)
XLA Ops:
  0.6 106.0 %shard_map.93 = (f32[3,5,32,128]{3,2,1,0:T(8,128)}, f32[3,32,128]{2,1,0:T(8,128)}, f32[6,6,32,128]{3,2,1,0:T(8,128)}, f32[6,32,128]{2,1,0:T(8,128)}) custom-call(s32[3,5]{1,0:T(4,128)} %st.1, f32[6,24,32,128]{3,2,1,0:T(8,128)} %g_in.1, f32[15,32,128]{2,1,0:T(8,128)} %bitcast.1, f32[3,32,128]{2,1,0:T(8,128)} %piv1.1, f32[6,6,32,128]{3,2,1,0:T(8,128)} %low2.1, ...), custom_call_target="tpu_custom_call" | custom-call | tf_op jit(solution)/shard_map/pallas_call | solution.py:603
  106.6 2.2 %shard_map.94 = (f32[3,5,32,128]{3,2,1,0:T(8,128)}, f32[3,32,128]{2,1,0:T(8,128)}, f32[6,6,32,128]{3,2,1,0:T(8,128)}, f32[6,32,128]{2,1,0:T(8,128)}) custom-call(f32[3,5,32,128]{3,2,1,0:T(8,128)} %get-tuple-element.8.refs_0_, f32[3,32,128]{2,1,0:T(8,128)} %get-tuple-element.9.refs_1_, f32[6,6,32,128]{3,2,1,0:T(8,128)} %get-tuple-element.10.refs_2_, ...), custom_call_target="tpu_custom_call" | custom-call | tf_op jit(solution)/shard_map/pallas_call | solution.py:654

commit v4 on v2

--- a/solution.py
+++ b/solution.py
@@ -54,7 +54,7 @@
     off1_out, diag1_out, off2_out, diag2_out,
     off1, diag1, off2, diag2,
     gv, av, p2, sv, xl, xb, xa, x3, zb, zl, za, ysel, yo, yn,
-    zacc0, zacc1, pb, gp, sr, send_r, send_l, in_r, in_l,
+    zacc, pb, gp, sr, send_r, send_l, in_r, in_l,
     sm, ssem, rsem, lsem, msem, osem,
 ):
     y = lax.axis_index("leaf")
@@ -291,46 +291,58 @@
             za[r, j] = fixed
             pb[j] = part[SK * TR :]
 
-    def multiply(j):
-        m, c = j // NC, j % NC
-        zacc = zacc1 if c else zacc0
-        zacc[...] = jnp.zeros_like(zacc)
-
-        def block(q, carry):
-            lhs = wide([x3[i, m, pl.ds(q * SK, SK)] for i in range(NX)])
-            rhs = tall(za[:, j, q])
-            if c == 0:
-                rhs = jnp.concatenate([tall(zl[:, m * SK + q]), rhs], axis=1)
-            zacc[...] += dot3(lhs, rhs, 1)
-            return carry
-
-        lax.fori_loop(0, SK, block, 0)
-        own = zacc[:, (1 - c) * TC : (2 - c) * TC] if c == 0 else zacc[...]
-        left = dot3(low_cols(m), zacc[...], 0)
-        parts = [left[:, b * TC : (b + 1) * TC] for b in range(2 - c)]
-        lhs = jnp.concatenate(
-            [
-                wide([xa[i, m, c * SK : (c + 1) * SK] for i in range(NX)]),
-                wide([xb[i, j] for i in range(NX)]),
-            ],
-            axis=0,
-        )
-        parts.append(dot3(lhs, jnp.concatenate([own, pb[j]], axis=0), 0))
+    def spread(j, parts):
         for b, part in enumerate(parts):
             tiles = part.reshape(NZ, 2, TR, TC)
             for hh in range(2):
                 gp[hh, j, :, b] = tiles[:, hh]
         reduces[j].share()
-        off2[j, 0:SK] = -own.reshape(SK, TR, TC)
+
+    def multiply(m):
+        acc = zacc.at[m]
+        acc[...] = jnp.zeros(acc.shape, F32)
+
+        def block(q, carry):
+            lhs = wide([x3[i, m, pl.ds(q * SK, SK)] for i in range(NX)])
+            rhs = jnp.concatenate(
+                [tall(zl[:, m * SK + q])]
+                + [tall(za[:, m * NC + c, q]) for c in range(NC)],
+                axis=1,
+            )
+            acc[...] += dot3(lhs, rhs, 1)
+            return carry
+
+        lax.fori_loop(0, SK, block, 0)
+        left = dot3(low_cols(m), acc[...], 0)
+        spread(2 * m, [left[:, b * TC : (b + 1) * TC] for b in range(1 + NC)])
+        off1[m] = -acc[:, 0:TC].reshape(SK, TR, TC)
+        store(off1.at[m], off1_out.at[m])
         upper = pl.ds(0, SK)
-        store(off2.at[j, upper], off2_out.at[j, upper])
-        if c == 0:
-            off1[m] = -zacc[:, 0:TC].reshape(SK, TR, TC)
-            store(off1.at[m], off1_out.at[m])
+        for c in range(NC):
+            j = m * NC + c
+            off2[j, 0:SK] = -acc[:, (c + 1) * TC : (c + 2) * TC].reshape(SK, TR, TC)
+            store(off2.at[j, upper], off2_out.at[j, upper])
+
+    def multiply_own(m):
+        parts = []
+        for c in range(NC):
+            j = m * NC + c
+            lhs = jnp.concatenate(
+                [
+                    wide([xa[i, m, c * SK : (c + 1) * SK] for i in range(NX)]),
+                    wide([xb[i, j] for i in range(NX)]),
+                ],
+                axis=0,
+            )
+            rhs = jnp.concatenate(
+                [zacc[m, :, (c + 1) * TC : (c + 2) * TC], pb[j]], axis=0
+            )
+            parts.append(dot3(lhs, rhs, 0))
+        spread(2 * m + 1, parts)
 
     class Reduce:
         def __init__(self, j):
-            self.j, self.m, self.c = j, j // NC, j % NC
+            self.j, self.m, self.c = j, j // 2, j % 2
             self.n = 3 - self.c
             self.half = 1 if self.c or self.m % 2 else 2
 
@@ -393,184 +405,187 @@
             total = in_r[j, 3, 0:n] + in_l[j, 3, 0:n] + self.mine(z)
             if c == 0:
                 diag1[m] = xl[x, NL + m] + total[0]
-            off2[j, SK] = total[n - 2] - pb[j]
-            diag2[j] = p2[j] + total[n - 1]
-
-    reduces = [Reduce(j) for j in range(NJ)]
+                for i in range(NC):
+                    off2[m * NC + i, SK] = total[1 + i] - pb[m * NC + i]
+            else:
+                for i in range(NC):
+                    diag2[m * NC + i] = p2[m * NC + i] + total[i]
+
+    reduces = [Reduce(j) for j in range(2 * NM)]
 
     for c in loads:
         c.wait()
 
-    x_lp.start()
+    send_lists()
     z_b[0].start()
-    send_lists()
     z_l[0].start()
     z_b[1].start()
-    z_b[2].start()
-    z_b[0].step(1)
-    x_b.start()
+    x_lp.start()
+    z_l[1].start()
     take_lists()
     y_far_half(0)
-    select(0, 0)
-    select(0, 3)
+    z_b[0].step(1)
+    z_b[2].start()
+    z_b[1].step(1)
+    z_l[0].step(1)
+    select(0, 4)
     y_near_half(0)
-    z_b[1].step(1)
+    x_b.start()
+    select(0, 5)
     z_b[2].step(1)
     z_b[0].step(2)
-    select(0, 2)
-    select(0, 5)
-    z_l[0].step(1)
-    select(0, 4)
-    x_lp.second()
-    z_b[1].step(2)
     y_merge(0)
     y_far_half(1)
+    x_lp.second()
+    z_l[2].start()
+    z_b[1].step(2)
     y_near_half(1)
+    x_b.second()
+    z_b[2].step(2)
     z_b[0].step(3)
-    z_l[1].start()
-    z_l[2].start()
-    x_b.second()
+    select(0, 0)
     z_l[0].step(2)
+    select(0, 1)
+    y_last(0)
+    z_l[2].step(1)
+    select(0, 3)
+    z_b[0].last()
     z_b[1].step(3)
-    z_b[2].step(2)
-    z_b[0].last()
-    y_last(0)
-    z_b[0].finish()
     z_l[1].step(1)
-    x_lp.finish()
-    x_b.finish()
-    correct(0)
-    z_a[0].start()
-    z_a[1].start()
     y_merge(1)
     y_far_half(2)
-    select(0, 1)
+    z_b[0].finish()
+    x_lp.finish()
+    correct(0)
+    z_a[1].start()
+    z_a[0].start()
+    x_a[0].start()
+    z_b[1].last()
     y_near_half(2)
-    x_a[0].start()
     z_l[0].step(3)
-    z_b[1].last()
     z_b[2].step(3)
+    y_last(1)
+    z_l[1].step(2)
     z_b[1].finish()
     correct(1)
-    x_a[1].start()
-    z_a[3].start()
-    z_l[1].step(2)
-    y_last(1)
-    x_s[0].second()
     z_a[2].start()
-    z_l[2].step(1)
-    z_a[0].step(1)
     y_merge(2)
     y_far_half(3)
+    z_a[0].step(1)
+    select(0, 2)
+    x_a[1].start()
+    z_b[2].last()
+    x_s[0].second()
+    z_a[1].step(1)
+    z_l[0].last()
+    z_a[3].start()
+    z_b[2].finish()
+    z_a[2].step(1)
+    z_l[1].step(3)
     y_near_half(3)
-    z_a[1].step(1)
+    y_last(2)
+    y_merge(3)
+    z_a[1].step(2)
+    y_far_half(4)
+    x_a[1].second()
+    z_a[0].step(2)
+    z_a[2].step(2)
+    correct(2)
+    y_near_half(4)
+    y_last(3)
+    z_a[5].start()
+    x_s[2].second()
+    z_l[0].finish()
+    z_a[4].start()
+    x_s[1].second()
+    z_a[3].step(1)
+    y_merge(4)
+    z_a[1].step(3)
+    y_far_half(5)
     x_a[0].second()
-    z_b[2].last()
-    z_b[2].finish()
-    correct(2)
+    y_near_half(5)
+    z_a[2].step(3)
+    z_a[0].step(3)
+    x_b.finish()
+    z_a[5].step(1)
+    y_last(4)
+    z_l[1].last()
+    z_a[1].last()
+    z_a[3].step(2)
+    x_s[2].finish()
+    x_s[0].finish()
+    z_a[4].step(1)
+    y_merge(5)
+    z_l[2].step(2)
+    z_a[0].last()
+    z_a[0].finish()
+    z_a[2].last()
+    x_s[1].finish()
+    z_a[1].finish()
+    x_s[3].second()
+    z_a[5].step(2)
+    x_a[0].finish()
+    multiply(0)
+    z_a[3].step(3)
+    y_last(5)
     x_a[2].start()
-    z_a[5].start()
-    z_a[3].step(1)
-    z_l[0].last()
-    x_a[1].second()
-    z_l[0].finish()
-    z_l[1].step(3)
-    y_last(2)
-    z_a[4].start()
-    z_a[2].step(1)
-    y_merge(3)
-    y_far_half(4)
-    y_near_half(4)
-    x_s[1].second()
-    z_l[2].step(2)
-    z_a[0].step(2)
-    x_s[0].finish()
-    z_a[1].step(2)
-    x_a[0].finish()
-    z_a[5].step(1)
-    y_last(3)
-    y_merge(4)
-    y_far_half(5)
-    y_near_half(5)
-    z_a[3].step(2)
-    z_l[1].last()
+    z_l[1].finish()
+    reduces[0].start()
+    multiply_own(0)
+    z_a[4].step(2)
+    z_l[2].step(3)
+    reduces[1].start()
+    x_s[4].second()
+    reduces[0].step(1)
+    z_a[5].step(3)
+    z_a[3].last()
+    z_a[3].finish()
+    z_a[2].finish()
+    x_s[5].second()
+    reduces[1].step(1)
+    z_a[4].step(3)
+    x_s[3].finish()
+    multiply(1)
+    reduces[0].step(2)
     x_a[2].second()
+    z_l[2].last()
     x_a[1].finish()
-    z_l[1].finish()
-    z_a[4].step(1)
-    y_last(4)
-    z_l[2].step(3)
-    y_merge(5)
-    z_a[0].step(3)
-    x_s[1].finish()
-    z_a[1].step(3)
-    y_last(5)
-    z_a[5].step(2)
-    z_a[3].step(3)
-    z_a[4].step(2)
-    z_a[2].step(2)
-    z_l[2].last()
-    z_a[0].last()
-    x_a[2].finish()
-    z_a[1].last()
-    z_a[0].finish()
-    multiply(0)
-    z_a[1].finish()
-    x_s[4].second()
-    multiply(1)
-    reduces[0].start()
-    z_a[3].last()
+    multiply_own(1)
+    reduces[1].step(2)
+    z_a[4].last()
+    reduces[2].start()
+    reduces[3].start()
     z_l[2].finish()
-    x_s[2].second()
-    z_a[4].step(3)
-    z_a[3].finish()
-    reduces[1].start()
-    z_a[5].step(3)
-    x_s[5].second()
-    reduces[0].step(1)
-    z_a[2].step(3)
-    x_s[3].second()
-    z_a[4].last()
-    x_s[4].finish()
     z_a[5].last()
     z_a[4].finish()
-    reduces[1].step(1)
+    reduces[0].step(3)
     z_a[5].finish()
-    reduces[0].step(2)
-    x_s[2].finish()
-    z_a[2].last()
-    z_a[2].finish()
-    reduces[1].step(2)
+    x_s[4].finish()
     x_s[5].finish()
-    multiply(5)
-    multiply(4)
-    reduces[0].step(3)
+    multiply(2)
+    x_a[2].finish()
+    reduces[3].step(1)
+    multiply_own(2)
+    reduces[4].start()
     reduces[5].start()
-    x_s[3].finish()
-    multiply(2)
-    reduces[4].start()
+    reduces[2].step(1)
+    reduces[3].step(2)
+    reduces[4].step(1)
+    reduces[5].step(1)
+    reduces[2].step(2)
     reduces[1].step(3)
-    multiply(3)
-    reduces[2].start()
-    reduces[0].finish()
-    reduces[3].start()
-    reduces[4].step(1)
-    reduces[1].finish()
-    reduces[5].step(1)
-    reduces[2].step(1)
-    reduces[3].step(1)
     reduces[4].step(2)
     reduces[5].step(2)
-    reduces[2].step(2)
-    reduces[3].step(2)
+    reduces[0].finish()
+    reduces[2].step(3)
+    reduces[3].step(3)
     reduces[4].step(3)
     reduces[5].step(3)
-    reduces[2].step(3)
-    reduces[3].step(3)
+    reduces[3].finish()
+    reduces[1].finish()
     reduces[4].finish()
+    reduces[2].finish()
     reduces[5].finish()
-    reduces[2].finish()
-    reduces[3].finish()
 
     last_row = pl.ds(SK, 1)
     store(off2.at[:, last_row], off2_out.at[:, last_row])
@@ -624,8 +639,7 @@
             vmem(NY, NM, BLK),
             vmem(NM, BLK),
             vmem(NM, 2, BLK),
-            pltpu.VMEM((SK * TR, 2 * TC), F32),
-            pltpu.VMEM((SK * TR, TC), F32),
+            pltpu.VMEM((NM, SK * TR, (1 + NC) * TC), F32),
             vmem(NJ),
             vmem(2, NJ, NZ, GT),
             vmem(NJ, NZ, GT),

time: 111 us -> 105 us (0.946)
  Pallas kernels: 111 us -> 105 us
    pallas_call x1, Pallas kernels: 108 us -> 103 us  [on_device(): pl.pallas_call(kernel, out_shape=outs, in_specs=[pl.BlockSpec(memory_spac...]
where the time goes in v4:
time: 105 us
  Pallas kernels  105 us (100%)
    pallas_call x1, Pallas kernels, on_device(): pl.pallas_call(kernel, out_shape=outs, in_specs=[pl.BlockSpec(memory_spac...  103 us
    pallas_call x1, Pallas kernels, on_device(): pl.pallas_call(hand_over, out_shape=outs, in_specs=[whole] * 4, out_specs...  2.16 us

profile of v4, /device:TPU:1, one launch (start us, length us, event | category | flops | bytes accessed | tf_op | source)
XLA Modules:
  0.0 105.3 jit_solution(4312024622483960630)
XLA Ops:
  0.6 102.5 %shard_map.93 = (f32[3,5,32,128]{3,2,1,0:T(8,128)}, f32[3,32,128]{2,1,0:T(8,128)}, f32[6,6,32,128]{3,2,1,0:T(8,128)}, f32[6,32,128]{2,1,0:T(8,128)}) custom-call(s32[3,5]{1,0:T(4,128)} %st.1, f32[6,24,32,128]{3,2,1,0:T(8,128)} %g_in.1, f32[15,32,128]{2,1,0:T(8,128)} %bitcast.1, f32[3,32,128]{2,1,0:T(8,128)} %piv1.1, f32[6,6,32,128]{3,2,1,0:T(8,128)} %low2.1, ...), custom_call_target="tpu_custom_call" | custom-call | tf_op jit(solution)/shard_map/pallas_call | solution.py:618
  103.2 2.2 %shard_map.94 = (f32[3,5,32,128]{3,2,1,0:T(8,128)}, f32[3,32,128]{2,1,0:T(8,128)}, f32[6,6,32,128]{3,2,1,0:T(8,128)}, f32[6,32,128]{2,1,0:T(8,128)}) custom-call(f32[3,5,32,128]{3,2,1,0:T(8,128)} %get-tuple-element.8.refs_0_, f32[3,32,128]{2,1,0:T(8,128)} %get-tuple-element.9.refs_1_, f32[6,6,32,128]{3,2,1,0:T(8,128)} %get-tuple-element.10.refs_2_, ...), custom_call_target="tpu_custom_call" | custom-call | tf_op jit(solution)/shard_map/pallas_call | solution.py:668

commit v5 on v4

--- a/solution.py
+++ b/solution.py
@@ -27,7 +27,7 @@
 HALF = (7, 6)
 GT = 3
 N_OUT = 42
-N_IN = 220
+N_IN = 130
 N_LOADS = 8
 N_STORES = NM + NJ + 3
 
@@ -129,51 +129,56 @@
         def __init__(self, at, n, half):
             self.at, self.n, self.half = at, n, half
 
+        def both(self, a, b):
+            self.into = next_in()
+            send(a, a, x_right, self.out, self.into)
+            send(b, b, x_left, self.out, self.into)
+
         def start(self):
             self.out = next_out(self.at(pl.ds(0, 3)))
-            own = self.at(x)
-            self.a = send(own, own, x_right, self.out, next_in())
-            self.b = send(own, own, x_left, self.out, next_in())
+            self.both(self.at(x), self.at(x))
 
         def second(self):
-            self.a.wait_recv()
-            a = self.at(wrap(x - 1, NX)).at[pl.ds(0, self.half)]
-            self.a = send(a, a, x_right, self.out, next_in())
-            self.b.wait_recv()
-            b = self.at(wrap(x + 1, NX)).at[pl.ds(self.half, self.n - self.half)]
-            self.b = send(b, b, x_left, self.out, next_in())
+            take(self.at(pl.ds(0, 2)), self.into)
+            self.both(
+                self.at(wrap(x - 1, NX)).at[pl.ds(0, self.half)],
+                self.at(wrap(x + 1, NX)).at[pl.ds(self.half, self.n - self.half)],
+            )
 
         def finish(self):
-            self.a.wait_recv()
-            self.b.wait_recv()
+            take(self.at(pl.ds(0, 1)), self.into)
 
     class ZRing:
         def __init__(self, at, n, half):
             self.at, self.n, self.half = at, n, half
+
+        def both(self, a, b):
+            self.into = next_in()
+            send(a, a, z_right, self.out, self.into)
+            send(b, b, z_left, self.out, self.into)
 
         def start(self):
             self.out = next_out(self.at(pl.ds(0, 2 * NZ - 1)))
             self.sib = next_in()
             own = self.at(r)
-            self.a = send(own, own, z_right, self.out, next_in())
-            self.b = send(own, own, z_left, self.out, next_in())
+            self.both(own, own)
             send(own, own, sibling, self.out, self.sib)
 
         def step(self, i):
-            self.a.wait_recv()
-            a = self.at(zrow(z - i))
-            part = a.at[pl.ds(0, self.half)] if i == 3 else a
-            self.a = send(part, part, z_right, self.out, next_in())
-            self.b.wait_recv()
-            b = self.at(zrow(z + i))
-            part = b.at[pl.ds(self.half, self.n - self.half)] if i == 3 else b
-            self.b = send(part, part, z_left, self.out, next_in())
+            take(self.at(pl.ds(0, 2)), self.into)
+            a, b = self.at(zrow(z - i)), self.at(zrow(z + i))
+            if i < 3:
+                self.both(a, b)
+            else:
+                self.both(
+                    a.at[pl.ds(0, self.half)],
+                    b.at[pl.ds(self.half, self.n - self.half)],
+                )
             send(a, a, sibling, self.out, self.sib)
             send(b, b, sibling, self.out, self.sib)
 
         def last(self):
-            self.a.wait_recv()
-            self.b.wait_recv()
+            take(self.at(pl.ds(0, 1)), self.into)
             far = self.at(zrow(z + 4))
             send(far, far, sibling, self.out, self.sib)
 
@@ -362,46 +367,41 @@
                 next_in(),
             )
 
+        def both(self, s, right, left):
+            j = self.j
+            self.into = next_in()
+            send(
+                send_r.at[j, s, right], in_r.at[j, s, right], z_right, self.out, self.into
+            )
+            send(send_l.at[j, s, left], in_l.at[j, s, left], z_left, self.out, self.into)
+
+        def arrived(self, pieces):
+            take(gp.at[0, self.j, pl.ds(0, pieces), pl.ds(0, self.n)], self.into)
+
         def start(self):
             j, n, k = self.j, self.n, self.half
             self.out = next_out(gp.at[0, j, pl.ds(0, NZ - 1), pl.ds(0, n)])
             self.s.wait_recv()
-            a, b = pl.ds(0, k), pl.ds(k, n - k)
             send_r[j, 0, 0:k] = self.mine(z + 4, 0, k)
-            self.a = send(
-                send_r.at[j, 0, a], in_r.at[j, 0, a], z_right, self.out, next_in()
-            )
             send_l[j, 0, k:n] = self.mine(z - 4, k, n)
-            self.b = send(
-                send_l.at[j, 0, b], in_l.at[j, 0, b], z_left, self.out, next_in()
-            )
+            self.both(0, pl.ds(0, k), pl.ds(k, n - k))
 
         def step(self, s):
             j, n, k = self.j, self.n, self.half
-            every = pl.ds(0, n)
-            self.a.wait_recv()
+            self.arrived(1 if s == 1 else 2)
             if s == 1:
                 send_r[j, 1, 0:k] = in_r[j, 0, 0:k] + self.mine(z + 3, 0, k)
                 send_r[j, 1, k:n] = self.mine(z + 3, k, n)
-            else:
-                send_r[j, s, 0:n] = in_r[j, s - 1, 0:n] + self.mine(z + 4 - s)
-            self.a = send(
-                send_r.at[j, s, every], in_r.at[j, s, every], z_right, self.out, next_in()
-            )
-            self.b.wait_recv()
-            if s == 1:
                 send_l[j, 1, 0:k] = self.mine(z - 3, 0, k)
                 send_l[j, 1, k:n] = in_l[j, 0, k:n] + self.mine(z - 3, k, n)
             else:
+                send_r[j, s, 0:n] = in_r[j, s - 1, 0:n] + self.mine(z + 4 - s)
                 send_l[j, s, 0:n] = in_l[j, s - 1, 0:n] + self.mine(z - 4 + s)
-            self.b = send(
-                send_l.at[j, s, every], in_l.at[j, s, every], z_left, self.out, next_in()
-            )
+            self.both(s, pl.ds(0, n), pl.ds(0, n))
 
         def finish(self):
             j, m, c, n = self.j, self.m, self.c, self.n
-            self.a.wait_recv()
-            self.b.wait_recv()
+            self.arrived(2)
             total = in_r[j, 3, 0:n] + in_l[j, 3, 0:n] + self.mine(z)
             if c == 0:
                 diag1[m] = xl[x, NL + m] + total[0]

time: 105 us -> 105 us (level)
  no operation moved by 1% of the time
where the time goes in v5:
time: 105 us
  Pallas kernels  104 us (99%)
    pallas_call x1, Pallas kernels, on_device(): pl.pallas_call(kernel, out_shape=outs, in_specs=[pl.BlockSpec(memory_spac...  102 us
    pallas_call x1, Pallas kernels, on_device(): pl.pallas_call(hand_over, out_shape=outs, in_specs=[whole] * 4, out_specs...  2.16 us

profile of v5, /device:TPU:1, one launch (start us, length us, event | category | flops | bytes accessed | tf_op | source)
XLA Modules:
  0.0 104.9 jit_solution(7240756783057452612)
XLA Ops:
  0.6 102.1 %shard_map.93 = (f32[3,5,32,128]{3,2,1,0:T(8,128)}, f32[3,32,128]{2,1,0:T(8,128)}, f32[6,6,32,128]{3,2,1,0:T(8,128)}, f32[6,32,128]{2,1,0:T(8,128)}) custom-call(s32[3,5]{1,0:T(4,128)} %st.1, f32[6,24,32,128]{3,2,1,0:T(8,128)} %g_in.1, f32[15,32,128]{2,1,0:T(8,128)} %bitcast.1, f32[3,32,128]{2,1,0:T(8,128)} %piv1.1, f32[6,6,32,128]{3,2,1,0:T(8,128)} %low2.1, ...), custom_call_target="tpu_custom_call" | custom-call | tf_op jit(solution)/shard_map/pallas_call | solution.py:618
  102.7 2.2 %shard_map.94 = (f32[3,5,32,128]{3,2,1,0:T(8,128)}, f32[3,32,128]{2,1,0:T(8,128)}, f32[6,6,32,128]{3,2,1,0:T(8,128)}, f32[6,32,128]{2,1,0:T(8,128)}) custom-call(f32[3,5,32,128]{3,2,1,0:T(8,128)} %get-tuple-element.8.refs_0_, f32[3,32,128]{2,1,0:T(8,128)} %get-tuple-element.9.refs_1_, f32[6,6,32,128]{3,2,1,0:T(8,128)} %get-tuple-element.10.refs_2_, ...), custom_call_target="tpu_custom_call" | custom-call | tf_op jit(solution)/shard_map/pallas_call | solution.py:668
